TPU v7x, 32 devices: a whole 2x2x4 slice. The times are simulated.
32 devices in a mesh: slab: 8 (over z, x), cable: 4 (over y, core).
Axes of the slice: x: 2, y: 2, z: 4, core: 2. Of those that a mesh axis runs over, the one named last changes fastest.
Arguments:
- electric: float32 [3, 256, 128, 256], P(None, ('slab', 'cable')), may hold values from -6 to 6
- magnetic: float32 [3, 256, 128, 256], P(None, ('slab', 'cable')), may hold values from -6 to 6
- conductivity: float32 [256, 128, 256], P(('slab', 'cable')), may hold values from 0.02 to 0.8
- voltage: float32 [32, 32, 4096], P(None, None, ('slab', 'cable')), may hold values from -6 to 6
- current: float32 [32, 32, 4096], P(None, None, ('slab', 'cable')), may hold values from -6 to 6
- inverse_inductance: float32 [32, 32, 4096], P(None, None, ('slab', 'cable')), as said below
- inverse_capacitance: float32 [32, 32, 4096], P(None, None, ('slab', 'cable')), as said below
- tangent: float32 [3, 32, 4096], P(None, ('slab', 'cable')), may hold values from -4 to 4
- sample_cell: int32 [32, 4096], P(('slab', 'cable')), may hold values from 0 to 1023
- tube_length: int32 [4096], P(('slab', 'cable')), may hold values from 8 to 32
- junction_link: int32 [4096], P(('slab', 'cable')), may hold values from 0 to 127, as said below
Outputs:
- electric_new: float32 [3, 256, 128, 256], P(None, ('slab', 'cable'))
- magnetic_new: float32 [3, 256, 128, 256], P(None, ('slab', 'cable'))
- voltage_new: float32 [32, 32, 4096], P(None, None, ('slab', 'cable'))
- current_new: float32 [32, 32, 4096], P(None, None, ('slab', 'cable'))
Inputs may be any that keep to these rules, and one draw needn't show every extreme that they name: `junction_link`: every aligned block of 128 entries holds each of its values once. `inverse_inductance`: symmetric, with off-diagonal entries summing to about as much as the diagonal. `inverse_capacitance`: symmetric, with off-diagonal entries summing to about as much as the diagonal.
All inputs are finite; a program needn't handle non-finite values.
Results may differ from a plain program's by a relative error of at most 0.0001.
Values sent between devices are 32-bit elements; how exact they have to be, the bound alone decides.
A program may use at most 128 MiB of HBM per device.

v0:
```python
import functools

import jax
import jax.numpy as jnp
from jax import lax
from jax.experimental import pallas as pl
from jax.experimental.pallas import tpu as pltpu
from jax.sharding import PartitionSpec as P

COURANT = 0.5
LANES = 128
SUBLANES = 8
AXES = ("slab", "cable")


def passed_along(x, axis, by):
    peers = lax.axis_size(axis)
    pairs = [(i, i + by) for i in range(peers) if 0 <= i + by < peers]
    return lax.ppermute(x, axis, pairs)


def passed_round(value, axis, steps):
    count = lax.axis_size(axis)
    pairs = [(source, (source + steps) % count) for source in range(count)]
    return lax.ppermute(value, axis, pairs)


def params(*semantics):
    if semantics:
        return pltpu.CompilerParams(dimension_semantics=semantics)
    return pltpu.CompilerParams()


def whole_block(shape):
    rank = len(shape)
    return pl.BlockSpec(shape, lambda i: (0,) * rank)


def gather_kernel(cell_ref, tangent_ref, field_ref, drive_ref, picked_ref):
    step = pl.program_id(0)
    block_rows, nz = field_ref.shape[1], field_ref.shape[2]
    halves = nz // LANES
    trays = cell_ref.shape[0] // halves
    groups = trays // SUBLANES
    chunks = block_rows // SUBLANES

    @pl.when(step == 0)
    def _():
        picked_ref[...] = jnp.zeros_like(picked_ref)

    for half in range(halves):
        for group in range(groups):
            start = group * SUBLANES * halves + half
            cells = cell_ref[pl.ds(start, SUBLANES, stride=halves), :]
            low = cells % SUBLANES
            high = cells // SUBLANES - step * chunks
            slot = half * groups + group

            def pick(chunk, found):
                rows = pl.ds(pl.multiple_of(chunk * SUBLANES, SUBLANES), SUBLANES)
                hit = high == chunk
                out = []
                for k in range(3):
                    tile = field_ref[k, rows, half * LANES : (half + 1) * LANES]
                    value = jnp.take_along_axis(tile, low, axis=0)
                    out.append(jnp.where(hit, value, found[k]))
                return tuple(out)

            found = tuple(picked_ref[k, slot] for k in range(3))
            found = lax.fori_loop(0, chunks, pick, found, unroll=8)
            for k in range(3):
                picked_ref[k, slot] = found[k]

    @pl.when(step == pl.num_programs(0) - 1)
    def _():
        for half in range(halves):
            for group in range(groups):
                slot = half * groups + group
                where = pl.ds(group * SUBLANES * halves + half, SUBLANES, stride=halves)
                drive_ref[where, :] = (
                    tangent_ref[0, where, :] * picked_ref[0, slot]
                    + tangent_ref[1, where, :] * picked_ref[1, slot]
                    + tangent_ref[2, where, :] * picked_ref[2, slot]
                )


def gather_samples(electric, cells, tangent):
    _, depth, ny, nz = electric.shape
    rows = depth * ny
    steps = 4
    field = electric.reshape(3, rows, nz)
    return pl.pallas_call(
        gather_kernel,
        grid=(steps,),
        out_shape=jax.ShapeDtypeStruct(cells.shape, jnp.float32),
        in_specs=[
            whole_block(cells.shape),
            whole_block(tangent.shape),
            pl.BlockSpec((3, rows // steps, nz), lambda i: (0, i, 0)),
        ],
        out_specs=whole_block(cells.shape),
        scratch_shapes=[
            pltpu.VMEM((3, cells.shape[0] // SUBLANES, SUBLANES, LANES), jnp.float32)
        ],
        compiler_params=params("arbitrary"),
        name="gather_samples",
    )(cells, tangent, field)


def ahead(x, axis):
    extent = x.shape[axis]
    index = lax.broadcasted_iota(jnp.int32, x.shape, axis)
    return jnp.where(index == extent - 1, 0.0, pltpu.roll(x, extent - 1, axis)) - x


def behind(x, axis):
    index = lax.broadcasted_iota(jnp.int32, x.shape, axis)
    return x - jnp.where(index == 0, 0.0, pltpu.roll(x, 1, axis))


def magnetic_kernel(electric_ref, magnetic_ref, above_ref, new_ref, last_ref, next_ref):
    @pl.when(pl.program_id(0) == 0)
    def _():
        next_ref[...] = above_ref[:, 0]

    ex, ey, ez = electric_ref[0, 0], electric_ref[1, 0], electric_ref[2, 0]
    new_ref[0, 0] = magnetic_ref[0, 0] - COURANT * (ahead(ez, 0) - ahead(ey, 1))
    new_y = magnetic_ref[1, 0] - COURANT * (ahead(ex, 1) - (next_ref[1] - ez))
    new_z = magnetic_ref[2, 0] - COURANT * ((next_ref[0] - ey) - ahead(ex, 0))
    new_ref[1, 0] = new_y
    new_ref[2, 0] = new_z
    next_ref[0] = ey
    next_ref[1] = ez

    @pl.when(pl.program_id(0) == 0)
    def _():
        last_ref[0, 0] = new_y
        last_ref[1, 0] = new_z


def magnetic_step(electric, magnetic, above):
    _, depth, ny, nz = electric.shape
    layer = pl.BlockSpec((3, 1, ny, nz), lambda i: (0, depth - 1 - i, 0, 0))
    edge = (2, 1, ny, nz)
    return pl.pallas_call(
        magnetic_kernel,
        grid=(depth,),
        out_shape=[
            jax.ShapeDtypeStruct(magnetic.shape, jnp.float32),
            jax.ShapeDtypeStruct(edge, jnp.float32),
        ],
        in_specs=[layer, layer, whole_block(edge)],
        out_specs=[layer, whole_block(edge)],
        scratch_shapes=[pltpu.VMEM((2, ny, nz), jnp.float32)],
        compiler_params=params("arbitrary"),
        name="magnetic_step",
    )(electric, magnetic, above)


def contract(matrix_ref, vector_ref, finish):
    conductors, segments = vector_ref.shape[0], vector_ref.shape[1]
    tall = 32 if segments % 32 == 0 else SUBLANES
    wide = 4

    def block(i, carry):
        first = i * wide
        for start in range(0, segments, tall):
            rows = slice(start, start + tall)
            sums = [None] * wide
            for d in range(conductors):
                vector = vector_ref[d, rows, :]
                for j in range(wide):
                    term = matrix_ref[first + j, d : d + 1, :] * vector
                    sums[j] = term if d == 0 else sums[j] + term
            for j in range(wide):
                finish(first + j, rows, sums[j])
        return carry

    lax.fori_loop(0, conductors // wide, block, 0)


def line_positions(length_ref, segments):
    lanes = length_ref.shape[1]
    position = lax.broadcasted_iota(jnp.int32, (segments, lanes), 0)
    live = (position < length_ref[...]).astype(jnp.float32)
    last = (position == length_ref[...] - 1).astype(jnp.float32)
    return position, live, last


def set_push(volts_ref, drive_ref, push_ref, position):
    segments = volts_ref.shape[1]

    def one(d, carry):
        volts = volts_ref[d]
        following = jnp.where(
            position == segments - 1, 0.0, pltpu.roll(volts, segments - 1, 0)
        )
        push_ref[d] = following - volts - drive_ref[...]
        return carry

    lax.fori_loop(0, volts_ref.shape[0], one, 0, unroll=4)


def set_slope(amps_ref, slope_ref, position, inflow_ref=None):
    def one(d, carry):
        amps = amps_ref[d]
        edge = 0.0 if inflow_ref is None else inflow_ref[pl.ds(d, 1), :]
        slope_ref[d] = amps - jnp.where(position == 0, edge, pltpu.roll(amps, 1, 0))
        return carry

    lax.fori_loop(0, amps_ref.shape[0], one, 0, unroll=4)


def amps_substep(inductance_ref, push_ref, old_ref, new_ref, live, last, end_ref, slot):
    ends = {}

    def finish(c, rows, total):
        new = live[rows] * (old_ref[c, rows, :] - total)
        new_ref[c, rows, :] = new
        end = jnp.sum(new * last[rows], axis=0, keepdims=True)
        if rows.start > 0:
            end = end + end_ref[slot, pl.ds(c, 1), :]
        end_ref[slot, pl.ds(c, 1), :] = end

    contract(inductance_ref, push_ref, finish)


def volts_substep(capacitance_ref, slope_ref, old_ref, new_ref, live):
    def finish(c, rows, total):
        new_ref[c, rows, :] = live[rows] * (old_ref[c, rows, :] - total)

    contract(capacitance_ref, slope_ref, finish)


def first_lines_kernel(
    drive_ref, volts_ref, amps_ref, inductance_ref, capacitance_ref, length_ref,
    volts_out, amps_out, end_out, work_ref, mid_ref,
):
    position, live, last = line_positions(length_ref, volts_ref.shape[1])
    set_push(volts_ref, drive_ref, work_ref, position)
    amps_substep(inductance_ref, work_ref, amps_ref, mid_ref, live, last, end_out, 0)
    set_slope(mid_ref, work_ref, position)
    volts_substep(capacitance_ref, work_ref, volts_ref, volts_out, live)
    set_push(volts_out, drive_ref, work_ref, position)
    amps_substep(inductance_ref, work_ref, mid_ref, amps_out, live, last, end_out, 1)


def second_lines_kernel(
    drive_ref, volts_ref, amps_ref, inductance_ref, capacitance_ref, length_ref,
    volts_out, amps_out, end_out, total_out, work_ref,
):
    position, live, last = line_positions(length_ref, volts_ref.shape[1])
    set_slope(amps_ref, work_ref, position)
    volts_substep(capacitance_ref, work_ref, volts_ref, volts_out, live)
    set_push(volts_out, drive_ref, work_ref, position)
    amps_substep(inductance_ref, work_ref, amps_ref, amps_out, live, last, end_out, 0)
    total = amps_out[0]
    for c in range(1, amps_out.shape[0]):
        total = total + amps_out[c]
    total_out[...] = total


def feed(end, link):
    picked = []
    for start in range(0, end.shape[0], SUBLANES):
        rows = end[start : start + SUBLANES]
        picked.append(
            jnp.take_along_axis(rows, jnp.broadcast_to(link, rows.shape), axis=1)
        )
    return jnp.concatenate(picked, axis=0)


def apply_symmetric(matrix_ref, vector):
    total = matrix_ref[0] * vector[0:1]
    for d in range(1, vector.shape[0]):
        total = total + matrix_ref[d] * vector[d : d + 1]
    return total


def junction_kernel(
    end_ref, link_ref, inductance_ref, capacitance_ref, total_ref,
    induced_out, amps_shift_out, volts_shift_out,
):
    link = link_ref[...]
    volts0 = apply_symmetric(capacitance_ref, feed(end_ref[0], link))
    fed = apply_symmetric(capacitance_ref, feed(end_ref[1], link))
    amps0 = apply_symmetric(inductance_ref, volts0)
    spread = apply_symmetric(capacitance_ref, amps0)
    volts0 = volts0 - spread + fed
    volts1 = spread
    amps0 = amps0 + apply_symmetric(inductance_ref, volts0 - volts1)
    amps1 = apply_symmetric(inductance_ref, volts1)
    volts_shift_out[0] = volts0
    volts_shift_out[1] = volts1
    amps_shift_out[0] = amps0
    amps_shift_out[1] = amps1
    position = lax.broadcasted_iota(jnp.int32, total_ref.shape, 0)
    conductors = end_ref.shape[1]
    first = jnp.sum(amps0, axis=0, keepdims=True)
    second = jnp.sum(amps1, axis=0, keepdims=True)
    shift = jnp.where(position == 0, first, jnp.where(position == 1, second, 0.0))
    induced_out[...] = (total_ref[...] + shift) * (1.0 / conductors)


def last_lines_kernel(
    end_ref, link_ref, volts_ref, amps_ref, volts_shift_ref, amps_shift_ref,
    capacitance_ref, length_ref, volts_out, amps_out, work_ref, inflow_ref, mid_ref,
):
    position, live, _ = line_positions(length_ref, volts_ref.shape[1])
    inflow_ref[...] = feed(end_ref[0], link_ref[...])

    def shifted(shift_ref, d):
        row = pl.ds(d, 1)
        return jnp.where(
            position == 0, shift_ref[0, row, :],
            jnp.where(position == 1, shift_ref[1, row, :], 0.0),
        )

    def one(d, carry):
        amps_out[d] = amps_ref[d] + shifted(amps_shift_ref, d)
        mid_ref[d] = volts_ref[d] + shifted(volts_shift_ref, d)
        return carry

    lax.fori_loop(0, volts_ref.shape[0], one, 0, unroll=2)
    set_slope(amps_out, work_ref, position, inflow_ref)
    volts_substep(capacitance_ref, work_ref, mid_ref, volts_out, live)


def plain_call(kernel, outs, scratch, name, *operands):
    vmem = pl.BlockSpec(memory_space=pltpu.VMEM)
    return pl.pallas_call(
        kernel,
        out_shape=[jax.ShapeDtypeStruct(shape, jnp.float32) for shape in outs],
        in_specs=[vmem] * len(operands),
        out_specs=[vmem] * len(outs),
        scratch_shapes=[pltpu.VMEM(shape, jnp.float32) for shape in scratch],
        compiler_params=params(),
        name=name,
    )(*operands)


def electric_kernel(
    cell_ref, tangent_ref, induced_ref, electric_ref, magnetic_ref, conductivity_ref,
    below_ref, new_ref, prev_ref, merged_ref, tray_ref,
):
    step = pl.program_id(0)
    ny, nz = new_ref.shape[2], new_ref.shape[3]
    halves = nz // LANES
    trays = cell_ref.shape[0] // halves
    groups = trays // SUBLANES

    @pl.when(step == 0)
    def _():
        prev_ref[...] = below_ref[:, 0]
        for half in range(halves):
            where = pl.ds(half, trays, stride=halves)
            cells = cell_ref[where, :]
            tray_ref[half] = cells
            weights = [tangent_ref[k, where, :] * induced_ref[where, :] for k in range(3)]
            sums = [jnp.zeros_like(w) for w in weights]
            for tray in range(trays):
                same = cells == cells[tray : tray + 1]
                for k in range(3):
                    sums[k] = sums[k] + jnp.where(same, weights[k][tray : tray + 1], 0.0)
            for k in range(3):
                merged_ref[k, half] = sums[k]

    hx, hy, hz = magnetic_ref[0, 0], magnetic_ref[1, 0], magnetic_ref[2, 0]
    new_ref[0, 0] = behind(hz, 0) - behind(hy, 1)
    new_ref[1, 0] = behind(hx, 1) - (hz - prev_ref[1])
    new_ref[2, 0] = (hy - prev_ref[0]) - behind(hx, 0)
    prev_ref[0] = hy
    prev_ref[1] = hz

    for half in range(halves):
        lanes = slice(half * LANES, (half + 1) * LANES)

        def rows_of(chunk, carry):
            first = pl.multiple_of(chunk * SUBLANES, SUBLANES)
            rows = pl.ds(first, SUBLANES)
            here = (
                lax.broadcasted_iota(jnp.int32, (SUBLANES, LANES), 0) + first + step * ny
            )
            code = jnp.full((SUBLANES, LANES), trays, jnp.int32)
            for tray in range(trays):
                code = jnp.where(tray_ref[half, tray : tray + 1, :] == here, tray, code)
            low = code % SUBLANES
            group_of = code // SUBLANES
            sigma = conductivity_ref[0, rows, lanes]
            inverse = 1.0 / (1.0 + sigma)
            keep = (1.0 - sigma) * inverse
            curl = COURANT * inverse
            for k in range(3):
                deposit = jnp.zeros((SUBLANES, LANES), jnp.float32)
                for group in range(groups):
                    part = merged_ref[k, half, group * SUBLANES : (group + 1) * SUBLANES, :]
                    value = jnp.take_along_axis(part, low, axis=0)
                    deposit = jnp.where(group_of == group, value, deposit)
                new_ref[k, 0, rows, lanes] = keep * electric_ref[k, 0, rows, lanes] + curl * (
                    new_ref[k, 0, rows, lanes] - deposit
                )
            return carry

        lax.fori_loop(0, ny // SUBLANES, rows_of, 0, unroll=2)


def electric_step(electric, magnetic_new, conductivity, below, cells, tangent, induced):
    _, depth, ny, nz = electric.shape
    layer = pl.BlockSpec((3, 1, ny, nz), lambda i: (0, i, 0, 0))
    halves = nz // LANES
    trays = cells.shape[0] // halves
    return pl.pallas_call(
        electric_kernel,
        grid=(depth,),
        out_shape=jax.ShapeDtypeStruct(electric.shape, jnp.float32),
        in_specs=[
            whole_block(cells.shape),
            whole_block(tangent.shape),
            whole_block(induced.shape),
            layer,
            layer,
            pl.BlockSpec((1, ny, nz), lambda i: (i, 0, 0)),
            whole_block(below.shape),
        ],
        out_specs=layer,
        scratch_shapes=[
            pltpu.VMEM((2, ny, nz), jnp.float32),
            pltpu.VMEM((3, halves, trays, LANES), jnp.float32),
            pltpu.VMEM((halves, trays, LANES), jnp.int32),
        ],
        compiler_params=params("arbitrary"),
        name="electric_step",
    )(cells, tangent, induced, electric, magnetic_new, conductivity, below)


def local(
    electric,
    magnetic,
    conductivity,
    voltage,
    current,
    inverse_inductance,
    inverse_capacitance,
    tangent,
    sample_cell,
    tube_length,
    junction_link,
):
    conductors, segments, tubes = voltage.shape
    devices = lax.axis_size(AXES)
    own_segments = sample_cell.shape[0]
    cells = sample_cell.reshape(-1, LANES)
    steer = tangent.reshape(3, -1, LANES)
    length = tube_length[None, :]
    link = junction_link[None, :]
    lines = voltage.shape
    end = (conductors, tubes)

    above = passed_along(electric[1:3, 0:1], AXES, -1)
    drive_local = gather_samples(electric, cells, steer)
    drive = lax.all_to_all(
        drive_local.reshape(own_segments, devices, tubes), AXES, split_axis=1, concat_axis=0, tiled=True
    ).reshape(segments, tubes)
    magnetic_new, top = magnetic_step(electric, magnetic, above)
    below = passed_along(top, AXES, 1)

    volts, amps, ends = plain_call(
        first_lines_kernel, [lines, lines, (2,) + end], [lines, lines], "first_lines",
        drive, voltage, current, inverse_inductance, inverse_capacitance, length,
    )
    fed = passed_round(ends, "cable", 1)
    volts, amps, ends, total = plain_call(
        second_lines_kernel, [lines, lines, (1,) + end, (segments, tubes)], [lines],
        "second_lines",
        drive, volts, amps, inverse_inductance, inverse_capacitance, length,
    )
    fed_last = passed_round(ends, "cable", 1)
    induced, amps_shift, volts_shift = plain_call(
        junction_kernel, [(segments, tubes), (2,) + end, (2,) + end], [], "junction",
        fed, link, inverse_inductance, inverse_capacitance, total,
    )
    induced_local = lax.all_to_all(
        induced.reshape(segments, 1, tubes), AXES, split_axis=0, concat_axis=1, tiled=True
    ).reshape(-1, LANES)
    volts, amps = plain_call(
        last_lines_kernel, [lines, lines], [lines, end, lines], "last_lines",
        fed_last, link, volts, amps, volts_shift, amps_shift, inverse_capacitance, length,
    )
    electric_new = electric_step(
        electric, magnetic_new, conductivity, below, cells, steer, induced_local
    )
    return (electric_new, magnetic_new, volts, amps)


def solution(mesh):
    return jax.shard_map(
        local,
        mesh=mesh,
        in_specs=(
            P(None, AXES, None, None),
            P(None, AXES, None, None),
            P(AXES, None, None),
            P(None, None, AXES),
            P(None, None, AXES),
            P(None, None, AXES),
            P(None, None, AXES),
            P(None, AXES, None),
            P(AXES, None),
            P(AXES),
            P(AXES),
        ),
        out_specs=(
            P(None, AXES, None, None),
            P(None, AXES, None, None),
            P(None, None, AXES),
            P(None, None, AXES),
        ),
        check_vma=False,
    )
```

profile of v0, /device:TPU:0, one launch (start us, length us, event | category | flops | bytes accessed | tf_op | source)
XLA Modules:
  0.0 74.4 jit_solution(919173860040713393)
XLA Ops:
  0.6 1.0 %slice.3 = f32[2,1,128,256]{3,2,1,0:T(8,128)S(1)} slice(f32[3,8,128,256]{3,2,1,0:T(8,128)} %electric_ref.3), slice={[1:3], [0:1], [0:128], [0:256]} | slice | bytes 524288 | tf_op jit(solution)/shard_map/slice | solution.py:459
  1.6 1.3 %collective-permute-start.1 = (f32[2,1,128,256]{3,2,1,0:T(8,128)S(1)}, f32[2,1,128,256]{3,2,1,0:T(8,128)S(1)}, u32[]{:S(2)}, u32[]{:S(2)}) collective-permute-start(f32[2,1,128,256]{3,2,1,0:T(8,128)S(1)} %slice.3), channel_id=1, source_target_pairs={{1,0},{2,1},{3,2},{4,3},{5,4},{6,5},{7,6},{8,7},{9,8},{10,9},{11,1... | collective-permute-start | bytes 786440 | tf_op jit(solution)/shard_map/ppermute | solution.py:19
  2.9 2.1 %collective-permute-done.1.above_ref = f32[2,1,128,256]{3,2,1,0:T(8,128)S(1)} collective-permute-done((f32[2,1,128,256]{3,2,1,0:T(8,128)S(1)}, f32[2,1,128,256]{3,2,1,0:T(8,128)S(1)}, u32[]{:S(2)}, u32[]{:S(2)}) %collective-permute-start.1) | collective-permute-done | bytes 262176 | tf_op jit(solution)/shard_map/ppermute | solution.py:19
  5.0 0.0 copy-start
  5.0 0.7 copy-done
  5.7 7.4 %magnetic_step.1 = (f32[3,8,128,256]{3,2,1,0:T(8,128)}, f32[2,1,128,256]{3,2,1,0:T(8,128)}) custom-call(f32[3,8,128,256]{3,2,1,0:T(8,128)} %electric_ref.3, f32[3,8,128,256]{3,2,1,0:T(8,128)} %magnetic_ref.1, f32[2,1,128,256]{3,2,1,0:T(8,128)} %copy-done), custom_call_target="tpu_custom_call" | custom-call | tf_op jit(solution)/shard_map/magnetic_step/pallas_call | solution.py:145
  13.1 7.5 %collective-permute-start.2 = (f32[2,1,128,256]{3,2,1,0:T(8,128)}, f32[2,1,128,256]{3,2,1,0:T(8,128)S(1)}, u32[]{:S(2)}, u32[]{:S(2)}) collective-permute-start(f32[2,1,128,256]{3,2,1,0:T(8,128)} %get-tuple-element.24), channel_id=1, source_target_pairs={{0,1},{1,2},{2,3},{3,4},{4,5},{5,6},{6,7},{7,8},{8,9},{9,10},{10,1... | collective-permute-start | bytes 786440 | tf_op jit(solution)/shard_map/ppermute | solution.py:19
  20.7 3.9 %gather_samples.1 = f32[32,128]{1,0:T(8,128)} custom-call(s32[32,128]{1,0:T(8,128)} %bitcast.18, f32[3,32,128]{2,1,0:T(8,128)} %bitcast.14, f32[3,1024,256]{2,1,0:T(8,128)} %bitcast.13), custom_call_target="tpu_custom_call" | custom-call | tf_op jit(solution)/shard_map/gather_samples/pallas_call | solution.py:92
  24.6 13.8 %all_to_all.8 = f32[1,32,128]{2,0,1:T(1,128)} all-to-all(f32[1,32,128]{2,0,1:T(1,128)} %bitcast.21), channel_id=1, replica_groups=mesh['slab'=8,'cable'=4] {'slab','cable'}, dimensions={1} | all-to-all | bytes 32768 | tf_op jit(solution)/shard_map/all_to_all | solution.py:461
  38.4 7.0 %first_lines.1 = (f32[32,32,128]{2,1,0:T(8,128)}, f32[32,32,128]{2,1,0:T(8,128)}, f32[2,32,128]{2,1,0:T(8,128)}) custom-call(f32[32,128]{1,0:T(8,128)} %bitcast.16, f32[32,32,128]{2,1,0:T(8,128)} %volts_ref.1, f32[32,32,128]{2,1,0:T(8,128)} %amps_ref.1, f32[32,32,128]{2,1,0:T(8,128)} %inductance_ref.5, f32[32,32,128]{2,1,0:T(8,128)} %capacitance_ref.7, ...), custom_call_target="tpu_custom_call" | custom-call | tf_op jit(solution)/shard_map/first_lines/pallas_call | solution.py:331
  45.3 0.0 collective-permute-start
  45.3 5.4 %second_lines.1 = (f32[32,32,128]{2,1,0:T(8,128)}, f32[32,32,128]{2,1,0:T(8,128)}, f32[1,32,128]{2,1,0:T(8,128)}, f32[32,128]{1,0:T(8,128)}) custom-call(f32[32,128]{1,0:T(8,128)} %bitcast.17, f32[32,32,128]{2,1,0:T(8,128)} %get-tuple-element.19.volts_ref, f32[32,32,128]{2,1,0:T(8,128)} %get-tuple-element.20.amps_ref, f32[32,32,128]{2,1,0:T(8,128)} %inductance_ref.5, ...), custom_call_target="tpu_custom_call" | custom-call | tf_op jit(solution)/shard_map/second_lines/pallas_call | solution.py:331
  50.7 0.0 collective-permute-done.end_ref
  50.7 0.0 copy-start.3
  50.7 0.6 copy-done.3
  51.3 2.2 %junction.1 = (f32[32,128]{1,0:T(8,128)}, f32[2,32,128]{2,1,0:T(8,128)}, f32[2,32,128]{2,1,0:T(8,128)}) custom-call(f32[2,32,128]{2,1,0:T(8,128)} %copy-done.3, s32[1,128]{1,0:T(1,128)} %bitcast.26, f32[32,32,128]{2,1,0:T(8,128)} %inductance_ref.5, f32[32,32,128]{2,1,0:T(8,128)} %capacitance_ref.7, f32[32,128]{1,0:T(8,128)} %get-tuple-element.21.total_ref), custom_call_target="tpu_custom_call" | custom-call | tf_op jit(solution)/shard_map/junction/pallas_call | solution.py:331
  53.4 2.6 %all-to-all-start.1 = ((f32[32,1,128]{2,1,0:T(1,128)}), f32[32,1,128]{2,1,0:T(1,128)S(1)}, u32[]{:S(2)}, u32[]{:S(2)}) async-start(f32[32,1,128]{2,1,0:T(1,128)} %bitcast.22), calls=%async_computation.1 | async-start | bytes 32768 | tf_op jit(solution)/shard_map/all_to_all | solution.py:482
  56.0 0.3 collective-permute-start.3
  56.4 3.1 %collective-permute-done.3.end_ref = f32[1,32,128]{2,1,0:T(8,128)S(1)} collective-permute-done((f32[1,32,128]{2,1,0:T(8,128)}, f32[1,32,128]{2,1,0:T(8,128)S(1)}, u32[]{:S(2)}, u32[]{:S(2)}) %collective-permute-start.3) | collective-permute-done | bytes 16416 | tf_op jit(solution)/shard_map/ppermute | solution.py:25
  59.4 0.0 copy-start.4
  59.4 0.6 copy-done.4
  60.0 3.9 %last_lines.1 = (f32[32,32,128]{2,1,0:T(8,128)}, f32[32,32,128]{2,1,0:T(8,128)}) custom-call(f32[1,32,128]{2,1,0:T(8,128)} %copy-done.4, s32[1,128]{1,0:T(1,128)} %bitcast.27, f32[32,32,128]{2,1,0:T(8,128)} %get-tuple-element.26.volts_ref, f32[32,32,128]{2,1,0:T(8,128)} %get-tuple-element.27.amps_ref, f32[2,32,128]{2,1,0:T(8,128)} %get-tuple-element.28.volts_shift_ref, ...), custom_call_target="tpu_custom_call" | custom-call | tf_op jit(solution)/shard_map/last_lines/pallas_call | solution.py:331
  64.0 0.0 all-to-all-done.1
  64.0 0.0 copy-start.2
  64.0 0.0 collective-permute-done.2.below_ref
  64.0 0.0 copy-start.1
  64.0 0.6 copy-done.2
  64.6 0.1 copy-done.1
  64.7 9.7 %electric_step.1 = f32[3,8,128,256]{3,2,1,0:T(8,128)} custom-call(s32[32,128]{1,0:T(8,128)} %bitcast.19, f32[3,32,128]{2,1,0:T(8,128)} %bitcast.15, f32[32,128]{1,0:T(8,128)} %bitcast.20, f32[3,8,128,256]{3,2,1,0:T(8,128)} %electric_ref.3, f32[3,8,128,256]{3,2,1,0:T(8,128)} %get-tuple-element.15.magnetic_ref, f32[8,128,256]{2,1,0:T(8,128)} %conductivity_ref.1, ...), custom_call_target="tpu_custom_call" | custom-call | tf_op jit(solution)/shard_map/electric_step/pallas_call | solution.py:412
Async XLA Ops:
  1.6 3.4 %collective-permute-start.1 = (f32[2,1,128,256]{3,2,1,0:T(8,128)S(1)}, f32[2,1,128,256]{3,2,1,0:T(8,128)S(1)}, u32[]{:S(2)}, u32[]{:S(2)}) collective-permute-start(f32[2,1,128,256]{3,2,1,0:T(8,128)S(1)} %slice.3), channel_id=1, source_target_pairs={{1,0},{2,1},{3,2},{4,3},{5,4},{6,5},{7,6},{8,7},{9,8},{10,9},{11,1... | collective-permute-start | bytes 786440 | tf_op jit(solution)/shard_map/ppermute | solution.py:19
  5.0 0.7 copy-start
  13.1 50.9 %collective-permute-start.2 = (f32[2,1,128,256]{3,2,1,0:T(8,128)}, f32[2,1,128,256]{3,2,1,0:T(8,128)S(1)}, u32[]{:S(2)}, u32[]{:S(2)}) collective-permute-start(f32[2,1,128,256]{3,2,1,0:T(8,128)} %get-tuple-element.24), channel_id=1, source_target_pairs={{0,1},{1,2},{2,3},{3,4},{4,5},{5,6},{6,7},{7,8},{8,9},{9,10},{10,1... | collective-permute-start | bytes 786440 | tf_op jit(solution)/shard_map/ppermute | solution.py:19
  45.3 5.4 %collective-permute-start = (f32[2,32,128]{2,1,0:T(8,128)}, f32[2,32,128]{2,1,0:T(8,128)S(1)}, u32[]{:S(2)}, u32[]{:S(2)}) collective-permute-start(f32[2,32,128]{2,1,0:T(8,128)} %get-tuple-element.18), channel_id=1, source_target_pairs={{0,1},{1,2},{2,3},{3,0},{4,5},{5,6},{6,7},{7,4},{8,9},{9,10},{10,1... | collective-permute-start | bytes 98312 | tf_op jit(solution)/shard_map/ppermute | solution.py:25
  50.7 0.6 copy-start.3
  53.4 10.5 %all-to-all-start.1 = ((f32[32,1,128]{2,1,0:T(1,128)}), f32[32,1,128]{2,1,0:T(1,128)S(1)}, u32[]{:S(2)}, u32[]{:S(2)}) async-start(f32[32,1,128]{2,1,0:T(1,128)} %bitcast.22), calls=%async_computation.1 | async-start | bytes 32768 | tf_op jit(solution)/shard_map/all_to_all | solution.py:482
  56.0 3.4 %collective-permute-start.3 = (f32[1,32,128]{2,1,0:T(8,128)}, f32[1,32,128]{2,1,0:T(8,128)S(1)}, u32[]{:S(2)}, u32[]{:S(2)}) collective-permute-start(f32[1,32,128]{2,1,0:T(8,128)} %get-tuple-element.25), channel_id=1, source_target_pairs={{0,1},{1,2},{2,3},{3,0},{4,5},{5,6},{6,7},{7,4},{8,9},{9,10},{10,1... | collective-permute-start | bytes 49160 | tf_op jit(solution)/shard_map/ppermute | solution.py:25
  59.4 0.6 copy-start.4
  64.0 0.6 copy-start.2
  64.0 0.7 copy-start.1
where the time goes:
time: 75.1 us; the launch traced here: 74.4 us
  Pallas kernels  39.4 us (52%)
  blocking collectives  13.8 us (18%)
  starting transfers between devices  11.7 us (16%)
  waiting for transfers between devices  5.22 us (7%)
  local copies, waits for them, and re-layouts  3.59 us (5%)
    pallas_call x4, Pallas kernels, plain_call(): pl.pallas_call(kernel, out_shape=[jax.ShapeDtypeStruct(shape, jnp.float32...  18.4 us
    all_to_all x1, blocking collectives, local(): lax.all_to_all(drive_local.reshape(own_segments, devices, tubes), AXES, s...  13.8 us
    pallas_call x1, Pallas kernels, electric_step(): pl.pallas_call(electric_kernel, grid=(depth,), out_shape=jax.ShapeDtypeSt...  9.68 us
    ppermute x2, starting transfers between devices, passed_along(): return lax.ppermute(x, axis, pairs)  8.84 us
    pallas_call x1, Pallas kernels, magnetic_step(): pl.pallas_call(magnetic_kernel, grid=(depth,), out_shape=[jax.ShapeDtypeS...  7.36 us
    pallas_call x1, Pallas kernels, gather_samples(): pl.pallas_call(gather_kernel, grid=(steps,), out_shape=jax.ShapeDtypeStru...  3.92 us
    ppermute x2, waiting for transfers between devices, passed_round(): return lax.ppermute(value, axis, pairs)  3.09 us
    unnamed x10, local copies, waits for them, and re-layouts  2.61 us
  transfers between devices with their start and end apart: 5, of which 2 were waited for; matrix products, arithmetic and copies ran while one was open for 0% of the time, Pallas kernels for 30%

commit v1 on v0

--- a/solution.py
+++ b/solution.py
@@ -13,12 +13,6 @@
 AXES = ("slab", "cable")
 
 
-def passed_along(x, axis, by):
-    peers = lax.axis_size(axis)
-    pairs = [(i, i + by) for i in range(peers) if 0 <= i + by < peers]
-    return lax.ppermute(x, axis, pairs)
-
-
 def passed_round(value, axis, steps):
     count = lax.axis_size(axis)
     pairs = [(source, (source + steps) % count) for source in range(count)]
@@ -36,75 +30,229 @@
     return pl.BlockSpec(shape, lambda i: (0,) * rank)
 
 
-def gather_kernel(cell_ref, tangent_ref, field_ref, drive_ref, picked_ref):
-    step = pl.program_id(0)
-    block_rows, nz = field_ref.shape[1], field_ref.shape[2]
+def everyone(mesh_shape):
+    slabs, cables = mesh_shape
+    count = slabs * cables
+    me = lax.axis_index("slab") * cables + lax.axis_index("cable")
+    return count, me, lambda peer: (peer // cables, peer % cables)
+
+
+def greet_all(count, me, place):
+    barrier = pltpu.get_barrier_semaphore()
+
+    def greet(k, carry):
+        pl.semaphore_signal(
+            barrier, inc=1, device_id=place((me + k) % count),
+            device_id_type=pl.DeviceIdType.MESH,
+        )
+        return carry
+
+    lax.fori_loop(1, count, greet, 0)
+    return lambda: pl.semaphore_wait(barrier, count - 1)
+
+
+def row_exchange(count, me, place, send_ref, recv_ref, send_sem, recv_sem):
+    def outgoing(k):
+        peer = (me + k) % count
+        return pltpu.make_async_remote_copy(
+            src_ref=send_ref.at[peer], dst_ref=recv_ref.at[me],
+            send_sem=send_sem.at[k], recv_sem=recv_sem.at[k],
+            device_id=place(peer), device_id_type=pl.DeviceIdType.MESH,
+        )
+
+    def incoming(k):
+        peer = (me + count - k) % count
+        return pltpu.make_async_remote_copy(
+            src_ref=send_ref.at[peer], dst_ref=recv_ref.at[peer],
+            send_sem=send_sem.at[k], recv_sem=recv_sem.at[k],
+            device_id=place(peer), device_id_type=pl.DeviceIdType.MESH,
+        )
+
+    def start(k, carry):
+        outgoing(k).start()
+        return carry
+
+    def finish(k, carry):
+        outgoing(k).wait_send()
+        incoming(k).wait_recv()
+        return carry
+
+    return (
+        lambda: lax.fori_loop(1, count, start, 0),
+        lambda: lax.fori_loop(1, count, finish, 0),
+    )
+
+
+def edge_copy(count, me, place, by, src, dst, send_sem, recv_sem):
+    has_target = (me + by >= 0) & (me + by < count)
+    has_source = (me - by >= 0) & (me - by < count)
+    target = (me + by + count) % count
+    copy = pltpu.make_async_remote_copy(
+        src_ref=src, dst_ref=dst, send_sem=send_sem, recv_sem=recv_sem,
+        device_id=place(target), device_id_type=pl.DeviceIdType.MESH,
+    )
+
+    def start():
+        @pl.when(has_target)
+        def _():
+            copy.start()
+
+    def received():
+        @pl.when(has_source)
+        def _():
+            copy.wait_recv()
+
+        @pl.when(jnp.logical_not(has_source))
+        def _():
+            dst[...] = jnp.zeros(dst.shape, jnp.float32)
+
+    def sent():
+        @pl.when(has_target)
+        def _():
+            copy.wait_send()
+
+    return start, received, sent
+
+
+def opening_kernel(
+    mesh_shape, cell_ref, tangent_ref, electric_hbm, magnetic_hbm, volts_hbm, amps_hbm,
+    inductance_hbm, drive_out, above_out, below_out, pre_out,
+    field, top_field, volts_ref, amps_ref, inductance_ref, push_ref, flat_ref,
+    send_ref, recv_ref, above_ref, top_ref, below_ref,
+    load_sem, send_sem, recv_sem, edge_sem,
+):
+    depth, ny, nz = field.shape[1:]
+    count, me, place = everyone(mesh_shape)
+    loads = []
+    for i in range(depth):
+        loads.append(
+            pltpu.make_async_copy(electric_hbm.at[:, i], field.at[:, i], load_sem.at[i])
+        )
+    extra = [
+        (magnetic_hbm.at[pl.ds(1, 2), depth - 1], top_field),
+        (volts_hbm, volts_ref),
+        (amps_hbm, amps_ref),
+        (inductance_hbm, inductance_ref),
+    ]
+    for i, (src, dst) in enumerate(extra):
+        loads.append(pltpu.make_async_copy(src, dst, load_sem.at[depth + i]))
+    for load in loads:
+        load.start()
+    greeted = greet_all(count, me, place)
+
+    loads[0].wait()
+    greeted()
+    send_above, above_here, above_sent = edge_copy(
+        count, me, place, -1, field.at[pl.ds(1, 2), 0], above_ref,
+        edge_sem.at[0], edge_sem.at[1],
+    )
+    send_above()
+
     halves = nz // LANES
     trays = cell_ref.shape[0] // halves
     groups = trays // SUBLANES
-    chunks = block_rows // SUBLANES
-
-    @pl.when(step == 0)
-    def _():
-        picked_ref[...] = jnp.zeros_like(picked_ref)
-
+    found = {}
+    for layer in range(depth):
+        if layer > 0:
+            loads[layer].wait()
+        for half in range(halves):
+            for group in range(groups):
+                start = group * SUBLANES * halves + half
+                cells = cell_ref[pl.ds(start, SUBLANES, stride=halves), :]
+                low = cells & (SUBLANES - 1)
+                high = cells // SUBLANES - layer * (ny // SUBLANES)
+
+                def pick(chunk, found):
+                    rows = pl.ds(pl.multiple_of(chunk * SUBLANES, SUBLANES), SUBLANES)
+                    hit = high == chunk
+                    out = []
+                    for k in range(3):
+                        tile = field[k, layer, rows, half * LANES : (half + 1) * LANES]
+                        value = jnp.take_along_axis(tile, low, axis=0)
+                        out.append(jnp.where(hit, value, found[k]))
+                    return tuple(out)
+
+                empty = (jnp.zeros((SUBLANES, LANES), jnp.float32),) * 3
+                found[half, group] = lax.fori_loop(
+                    0, ny // SUBLANES, pick, found.get((half, group), empty), unroll=4
+                )
     for half in range(halves):
         for group in range(groups):
-            start = group * SUBLANES * halves + half
-            cells = cell_ref[pl.ds(start, SUBLANES, stride=halves), :]
-            low = cells % SUBLANES
-            high = cells // SUBLANES - step * chunks
-            slot = half * groups + group
-
-            def pick(chunk, found):
-                rows = pl.ds(pl.multiple_of(chunk * SUBLANES, SUBLANES), SUBLANES)
-                hit = high == chunk
-                out = []
-                for k in range(3):
-                    tile = field_ref[k, rows, half * LANES : (half + 1) * LANES]
-                    value = jnp.take_along_axis(tile, low, axis=0)
-                    out.append(jnp.where(hit, value, found[k]))
-                return tuple(out)
-
-            found = tuple(picked_ref[k, slot] for k in range(3))
-            found = lax.fori_loop(0, chunks, pick, found, unroll=8)
-            for k in range(3):
-                picked_ref[k, slot] = found[k]
-
-    @pl.when(step == pl.num_programs(0) - 1)
-    def _():
-        for half in range(halves):
-            for group in range(groups):
-                slot = half * groups + group
-                where = pl.ds(group * SUBLANES * halves + half, SUBLANES, stride=halves)
-                drive_ref[where, :] = (
-                    tangent_ref[0, where, :] * picked_ref[0, slot]
-                    + tangent_ref[1, where, :] * picked_ref[1, slot]
-                    + tangent_ref[2, where, :] * picked_ref[2, slot]
-                )
-
-
-def gather_samples(electric, cells, tangent):
+            where = pl.ds(group * SUBLANES * halves + half, SUBLANES, stride=halves)
+            x, y, z = found[half, group]
+            flat_ref[where, :] = (
+                tangent_ref[0, where, :] * x
+                + tangent_ref[1, where, :] * y
+                + tangent_ref[2, where, :] * z
+            )
+    for row in range(count):
+        send_ref[row] = flat_ref[row : row + 1, :]
+    start_rows, finish_rows = row_exchange(
+        count, me, place, send_ref, recv_ref, send_sem, recv_sem
+    )
+    start_rows()
+
+    loads[depth].wait()
+    above_here()
+    ex, ey, ez = field[0, depth - 1], field[1, depth - 1], field[2, depth - 1]
+    top_ref[0] = top_field[0] - COURANT * (ahead(ex, 1) - (above_ref[1] - ez))
+    top_ref[1] = top_field[1] - COURANT * ((above_ref[0] - ey) - ahead(ex, 0))
+    send_below, below_here, below_sent = edge_copy(
+        count, me, place, 1, top_ref, below_ref, edge_sem.at[2], edge_sem.at[3]
+    )
+    send_below()
+
+    for load in loads[depth + 1 :]:
+        load.wait()
+    position = lax.broadcasted_iota(jnp.int32, volts_ref.shape[1:], 0)
+    set_push(volts_ref, None, push_ref, position)
+
+    def keep(c, rows, total):
+        pre_out[c, rows, :] = amps_ref[c, rows, :] - total
+
+    contract(inductance_ref, push_ref, keep)
+
+    recv_ref[me] = flat_ref[pl.ds(me, 1), :]
+    above_out[:, 0] = above_ref[...]
+    finish_rows()
+    for row in range(count):
+        drive_out[row : row + 1, :] = recv_ref[row]
+    below_here()
+    below_out[:, 0] = below_ref[...]
+    above_sent()
+    below_sent()
+
+
+def opening(mesh_shape, cells, steer, electric, magnetic, volts, amps, inductance):
     _, depth, ny, nz = electric.shape
-    rows = depth * ny
-    steps = 4
-    field = electric.reshape(3, rows, nz)
+    count = mesh_shape[0] * mesh_shape[1]
+    assert cells.shape[0] == count
+    vmem = pl.BlockSpec(memory_space=pltpu.VMEM)
+    hbm = pl.BlockSpec(memory_space=pl.ANY)
+    lines = volts.shape
+    row = (count, 1, LANES)
+    edge = (2, 1, ny, nz)
+    scratch = [
+        (3, depth, ny, nz), (2, ny, nz), lines, lines, inductance.shape, lines,
+        cells.shape, row, row, edge[:1] + edge[2:], edge[:1] + edge[2:],
+        edge[:1] + edge[2:],
+    ]
+    outs = [(lines[1], lines[2]), edge, edge, lines]
     return pl.pallas_call(
-        gather_kernel,
-        grid=(steps,),
-        out_shape=jax.ShapeDtypeStruct(cells.shape, jnp.float32),
-        in_specs=[
-            whole_block(cells.shape),
-            whole_block(tangent.shape),
-            pl.BlockSpec((3, rows // steps, nz), lambda i: (0, i, 0)),
+        functools.partial(opening_kernel, mesh_shape),
+        out_shape=[jax.ShapeDtypeStruct(shape, jnp.float32) for shape in outs],
+        in_specs=[vmem, vmem] + [hbm] * 5,
+        out_specs=[vmem] * len(outs),
+        scratch_shapes=[pltpu.VMEM(shape, jnp.float32) for shape in scratch]
+        + [
+            pltpu.SemaphoreType.DMA((depth + 4,)),
+            pltpu.SemaphoreType.DMA((count,)),
+            pltpu.SemaphoreType.DMA((count,)),
+            pltpu.SemaphoreType.DMA((4,)),
         ],
-        out_specs=whole_block(cells.shape),
-        scratch_shapes=[
-            pltpu.VMEM((3, cells.shape[0] // SUBLANES, SUBLANES, LANES), jnp.float32)
-        ],
-        compiler_params=params("arbitrary"),
-        name="gather_samples",
-    )(cells, tangent, field)
+        compiler_params=pltpu.CompilerParams(collective_id=0, has_side_effects=True),
+        name="opening",
+    )(cells, steer, electric, magnetic, volts, amps, inductance)
 
 
 def ahead(x, axis):
@@ -116,45 +264,6 @@
 def behind(x, axis):
     index = lax.broadcasted_iota(jnp.int32, x.shape, axis)
     return x - jnp.where(index == 0, 0.0, pltpu.roll(x, 1, axis))
-
-
-def magnetic_kernel(electric_ref, magnetic_ref, above_ref, new_ref, last_ref, next_ref):
-    @pl.when(pl.program_id(0) == 0)
-    def _():
-        next_ref[...] = above_ref[:, 0]
-
-    ex, ey, ez = electric_ref[0, 0], electric_ref[1, 0], electric_ref[2, 0]
-    new_ref[0, 0] = magnetic_ref[0, 0] - COURANT * (ahead(ez, 0) - ahead(ey, 1))
-    new_y = magnetic_ref[1, 0] - COURANT * (ahead(ex, 1) - (next_ref[1] - ez))
-    new_z = magnetic_ref[2, 0] - COURANT * ((next_ref[0] - ey) - ahead(ex, 0))
-    new_ref[1, 0] = new_y
-    new_ref[2, 0] = new_z
-    next_ref[0] = ey
-    next_ref[1] = ez
-
-    @pl.when(pl.program_id(0) == 0)
-    def _():
-        last_ref[0, 0] = new_y
-        last_ref[1, 0] = new_z
-
-
-def magnetic_step(electric, magnetic, above):
-    _, depth, ny, nz = electric.shape
-    layer = pl.BlockSpec((3, 1, ny, nz), lambda i: (0, depth - 1 - i, 0, 0))
-    edge = (2, 1, ny, nz)
-    return pl.pallas_call(
-        magnetic_kernel,
-        grid=(depth,),
-        out_shape=[
-            jax.ShapeDtypeStruct(magnetic.shape, jnp.float32),
-            jax.ShapeDtypeStruct(edge, jnp.float32),
-        ],
-        in_specs=[layer, layer, whole_block(edge)],
-        out_specs=[layer, whole_block(edge)],
-        scratch_shapes=[pltpu.VMEM((2, ny, nz), jnp.float32)],
-        compiler_params=params("arbitrary"),
-        name="magnetic_step",
-    )(electric, magnetic, above)
 
 
 def contract(matrix_ref, vector_ref, finish):
@@ -195,7 +304,8 @@
         following = jnp.where(
             position == segments - 1, 0.0, pltpu.roll(volts, segments - 1, 0)
         )
-        push_ref[d] = following - volts - drive_ref[...]
+        push = following - volts
+        push_ref[d] = push if drive_ref is None else push - drive_ref[...]
         return carry
 
     lax.fori_loop(0, volts_ref.shape[0], one, 0, unroll=4)
@@ -233,12 +343,23 @@
 
 
 def first_lines_kernel(
-    drive_ref, volts_ref, amps_ref, inductance_ref, capacitance_ref, length_ref,
-    volts_out, amps_out, end_out, work_ref, mid_ref,
+    drive_ref, volts_ref, pre_ref, inductance_ref, capacitance_ref, length_ref,
+    volts_out, amps_out, end_out, work_ref, mid_ref, sum_ref,
 ):
     position, live, last = line_positions(length_ref, volts_ref.shape[1])
-    set_push(volts_ref, drive_ref, work_ref, position)
-    amps_substep(inductance_ref, work_ref, amps_ref, mid_ref, live, last, end_out, 0)
+    total = inductance_ref[0]
+    for d in range(1, inductance_ref.shape[0]):
+        total = total + inductance_ref[d]
+    sum_ref[...] = total
+
+    def driven(c, carry):
+        row = pl.ds(c, 1)
+        new = live * (pre_ref[c] + sum_ref[row, :] * drive_ref[...])
+        mid_ref[c] = new
+        end_out[0, row, :] = jnp.sum(new * last, axis=0, keepdims=True)
+        return carry
+
+    lax.fori_loop(0, pre_ref.shape[0], driven, 0, unroll=4)
     set_slope(mid_ref, work_ref, position)
     volts_substep(capacitance_ref, work_ref, volts_ref, volts_out, live)
     set_push(volts_out, drive_ref, work_ref, position)
@@ -341,17 +462,19 @@
 
 def electric_kernel(
     cell_ref, tangent_ref, induced_ref, electric_ref, magnetic_ref, conductivity_ref,
-    below_ref, new_ref, prev_ref, merged_ref, tray_ref,
+    above_ref, below_ref, new_ref, fresh_ref, prev_ref, held_ref, merged_ref, tray_ref,
 ):
-    step = pl.program_id(0)
+    turn = pl.program_id(0)
+    step = turn - 1
     ny, nz = new_ref.shape[2], new_ref.shape[3]
     halves = nz // LANES
     trays = cell_ref.shape[0] // halves
     groups = trays // SUBLANES
 
-    @pl.when(step == 0)
+    @pl.when(turn == 0)
     def _():
         prev_ref[...] = below_ref[:, 0]
+        held_ref[...] = electric_ref[:, 0]
         for half in range(halves):
             where = pl.ds(half, trays, stride=halves)
             cells = cell_ref[where, :]
@@ -365,75 +488,90 @@
             for k in range(3):
                 merged_ref[k, half] = sums[k]
 
-    hx, hy, hz = magnetic_ref[0, 0], magnetic_ref[1, 0], magnetic_ref[2, 0]
-    new_ref[0, 0] = behind(hz, 0) - behind(hy, 1)
-    new_ref[1, 0] = behind(hx, 1) - (hz - prev_ref[1])
-    new_ref[2, 0] = (hy - prev_ref[0]) - behind(hx, 0)
-    prev_ref[0] = hy
-    prev_ref[1] = hz
-
-    for half in range(halves):
-        lanes = slice(half * LANES, (half + 1) * LANES)
-
-        def rows_of(chunk, carry):
-            first = pl.multiple_of(chunk * SUBLANES, SUBLANES)
-            rows = pl.ds(first, SUBLANES)
-            here = (
-                lax.broadcasted_iota(jnp.int32, (SUBLANES, LANES), 0) + first + step * ny
-            )
-            code = jnp.full((SUBLANES, LANES), trays, jnp.int32)
-            for tray in range(trays):
-                code = jnp.where(tray_ref[half, tray : tray + 1, :] == here, tray, code)
-            low = code % SUBLANES
-            group_of = code // SUBLANES
-            sigma = conductivity_ref[0, rows, lanes]
-            inverse = 1.0 / (1.0 + sigma)
-            keep = (1.0 - sigma) * inverse
-            curl = COURANT * inverse
-            for k in range(3):
-                deposit = jnp.zeros((SUBLANES, LANES), jnp.float32)
-                for group in range(groups):
-                    part = merged_ref[k, half, group * SUBLANES : (group + 1) * SUBLANES, :]
-                    value = jnp.take_along_axis(part, low, axis=0)
-                    deposit = jnp.where(group_of == group, value, deposit)
-                new_ref[k, 0, rows, lanes] = keep * electric_ref[k, 0, rows, lanes] + curl * (
-                    new_ref[k, 0, rows, lanes] - deposit
+    @pl.when(turn > 0)
+    def _():
+        final = turn == pl.num_programs(0) - 1
+        next_y = jnp.where(final, above_ref[0, 0], electric_ref[1, 0])
+        next_z = jnp.where(final, above_ref[1, 0], electric_ref[2, 0])
+        ex, ey, ez = held_ref[0], held_ref[1], held_ref[2]
+        fresh_ref[0, 0] = magnetic_ref[0, 0] - COURANT * (ahead(ez, 0) - ahead(ey, 1))
+        fresh_ref[1, 0] = magnetic_ref[1, 0] - COURANT * (ahead(ex, 1) - (next_z - ez))
+        fresh_ref[2, 0] = magnetic_ref[2, 0] - COURANT * ((next_y - ey) - ahead(ex, 0))
+        hx, hy, hz = fresh_ref[0, 0], fresh_ref[1, 0], fresh_ref[2, 0]
+        new_ref[0, 0] = behind(hz, 0) - behind(hy, 1)
+        new_ref[1, 0] = behind(hx, 1) - (hz - prev_ref[1])
+        new_ref[2, 0] = (hy - prev_ref[0]) - behind(hx, 0)
+        prev_ref[0] = hy
+        prev_ref[1] = hz
+
+        for half in range(halves):
+            lanes = slice(half * LANES, (half + 1) * LANES)
+
+            def rows_of(chunk, carry):
+                first = pl.multiple_of(chunk * SUBLANES, SUBLANES)
+                rows = pl.ds(first, SUBLANES)
+                here = (
+                    lax.broadcasted_iota(jnp.int32, (SUBLANES, LANES), 0) + first + step * ny
                 )
-            return carry
-
-        lax.fori_loop(0, ny // SUBLANES, rows_of, 0, unroll=2)
-
-
-def electric_step(electric, magnetic_new, conductivity, below, cells, tangent, induced):
+                code = jnp.full((SUBLANES, LANES), trays, jnp.int32)
+                for tray in range(trays):
+                    code = jnp.where(tray_ref[half, tray : tray + 1, :] == here, tray, code)
+                low = code % SUBLANES
+                group_of = code // SUBLANES
+                sigma = conductivity_ref[0, rows, lanes]
+                inverse = 1.0 / (1.0 + sigma)
+                keep = (1.0 - sigma) * inverse
+                curl = COURANT * inverse
+                for k in range(3):
+                    deposit = jnp.zeros((SUBLANES, LANES), jnp.float32)
+                    for group in range(groups):
+                        part = merged_ref[k, half, group * SUBLANES : (group + 1) * SUBLANES, :]
+                        value = jnp.take_along_axis(part, low, axis=0)
+                        deposit = jnp.where(group_of == group, value, deposit)
+                    new_ref[k, 0, rows, lanes] = keep * held_ref[k, rows, lanes] + curl * (
+                        new_ref[k, 0, rows, lanes] - deposit
+                    )
+                return carry
+
+            lax.fori_loop(0, ny // SUBLANES, rows_of, 0, unroll=2)
+        held_ref[...] = electric_ref[:, 0]
+
+
+def field_step(electric, magnetic, conductivity, above, below, cells, tangent, induced):
     _, depth, ny, nz = electric.shape
-    layer = pl.BlockSpec((3, 1, ny, nz), lambda i: (0, i, 0, 0))
     halves = nz // LANES
     trays = cells.shape[0] // halves
+    layer = (3, 1, ny, nz)
+    leading = pl.BlockSpec(layer, lambda i: (0, jnp.minimum(i, depth - 1), 0, 0))
+    trailing = pl.BlockSpec(layer, lambda i: (0, jnp.maximum(i - 1, 0), 0, 0))
     return pl.pallas_call(
         electric_kernel,
-        grid=(depth,),
-        out_shape=jax.ShapeDtypeStruct(electric.shape, jnp.float32),
+        grid=(depth + 1,),
+        out_shape=[jax.ShapeDtypeStruct(electric.shape, jnp.float32)] * 2,
         in_specs=[
             whole_block(cells.shape),
             whole_block(tangent.shape),
             whole_block(induced.shape),
-            layer,
-            layer,
-            pl.BlockSpec((1, ny, nz), lambda i: (i, 0, 0)),
+            leading,
+            trailing,
+            pl.BlockSpec((1, ny, nz), lambda i: (jnp.maximum(i - 1, 0), 0, 0)),
+            whole_block(above.shape),
             whole_block(below.shape),
         ],
-        out_specs=layer,
+        out_specs=[trailing, trailing],
         scratch_shapes=[
             pltpu.VMEM((2, ny, nz), jnp.float32),
+            pltpu.VMEM((3, ny, nz), jnp.float32),
             pltpu.VMEM((3, halves, trays, LANES), jnp.float32),
             pltpu.VMEM((halves, trays, LANES), jnp.int32),
         ],
         compiler_params=params("arbitrary"),
-        name="electric_step",
-    )(cells, tangent, induced, electric, magnetic_new, conductivity, below)
+        name="field_step",
+    )(cells, tangent, induced, electric, magnetic, conductivity, above, below)
 
 
 def local(
+    mesh_shape,
     electric,
     magnetic,
     conductivity,
@@ -447,8 +585,6 @@
     junction_link,
 ):
     conductors, segments, tubes = voltage.shape
-    devices = lax.axis_size(AXES)
-    own_segments = sample_cell.shape[0]
     cells = sample_cell.reshape(-1, LANES)
     steer = tangent.reshape(3, -1, LANES)
     length = tube_length[None, :]
@@ -456,17 +592,12 @@
     lines = voltage.shape
     end = (conductors, tubes)
 
-    above = passed_along(electric[1:3, 0:1], AXES, -1)
-    drive_local = gather_samples(electric, cells, steer)
-    drive = lax.all_to_all(
-        drive_local.reshape(own_segments, devices, tubes), AXES, split_axis=1, concat_axis=0, tiled=True
-    ).reshape(segments, tubes)
-    magnetic_new, top = magnetic_step(electric, magnetic, above)
-    below = passed_along(top, AXES, 1)
-
+    drive, above, below, pre = opening(
+        mesh_shape, cells, steer, electric, magnetic, voltage, current, inverse_inductance
+    )
     volts, amps, ends = plain_call(
-        first_lines_kernel, [lines, lines, (2,) + end], [lines, lines], "first_lines",
-        drive, voltage, current, inverse_inductance, inverse_capacitance, length,
+        first_lines_kernel, [lines, lines, (2,) + end], [lines, lines, end], "first_lines",
+        drive, voltage, pre, inverse_inductance, inverse_capacitance, length,
     )
     fed = passed_round(ends, "cable", 1)
     volts, amps, ends, total = plain_call(
@@ -486,15 +617,16 @@
         last_lines_kernel, [lines, lines], [lines, end, lines], "last_lines",
         fed_last, link, volts, amps, volts_shift, amps_shift, inverse_capacitance, length,
     )
-    electric_new = electric_step(
-        electric, magnetic_new, conductivity, below, cells, steer, induced_local
+    electric_new, magnetic_new = field_step(
+        electric, magnetic, conductivity, above, below, cells, steer, induced_local
     )
     return (electric_new, magnetic_new, volts, amps)
 
 
 def solution(mesh):
+    mesh_shape = (mesh.shape["slab"], mesh.shape["cable"])
     return jax.shard_map(
-        local,
+        functools.partial(local, mesh_shape),
         mesh=mesh,
         in_specs=(
             P(None, AXES, None, None),

time: 75.1 us -> 59.2 us (0.79)
  blocking collectives: 13.8 us -> 0 us
  Pallas kernels: 39.4 us -> 43.7 us
  starting transfers between devices: 11.7 us -> 9.39 us
  waiting for transfers between devices: 5.22 us -> 3.13 us
  local copies, waits for them, and re-layouts: 3.59 us -> 1.8 us
    all_to_all x1 -> x0, blocking collectives: 13.8 us -> none  [local(): lax.all_to_all(drive_local.reshape(own_segments, devices, tubes), AXES, s...]
    ppermute x2 -> x0, starting transfers between devices: 8.84 us -> none  [passed_along(): return lax.ppermute(x, axis, pairs)]
    pallas_call x3 -> x2, Pallas kernels: 21 us -> 26.6 us  [the longest x1 15.2 us: opening(): pl.pallas_call(functools.partial(opening_kernel, mesh_shape), out_shape=[...]
    all_to_all x1, starting transfers between devices: 2.55 us -> 6.17 us  [local(): lax.all_to_all(induced.reshape(segments, 1, tubes), AXES, split_axis=0, c...]
    ppermute x2, starting transfers between devices: 0.35 us -> 3.22 us  [passed_round(): return lax.ppermute(value, axis, pairs)]
    ppermute x2 -> x0, waiting for transfers between devices: 2.13 us -> none  [passed_along(): return lax.ppermute(x, axis, pairs)]
    pallas_call x4, Pallas kernels: 18.4 us -> 17.1 us  [plain_call(): pl.pallas_call(kernel, out_shape=[jax.ShapeDtypeStruct(shape, jnp.float32...]
    slice x1 -> x0, local copies, waits for them, and re-layouts: 0.98 us -> none  [local(): above = passed_along(electric[1:3, 0:1], AXES, -1)]
  transfers between devices with their start and end apart: 5 -> 3, of which waited for: 2 -> 1; matrix products, arithmetic and copies ran while one was open for 0% -> 0% of each run, Pallas kernels for 30% -> 16%
where the time goes in v1:
time: 59.2 us; the launch traced here: 58.6 us
  Pallas kernels  43.7 us (74%)
  starting transfers between devices  9.39 us (16%)
  waiting for transfers between devices  3.13 us (5%)
  local copies, waits for them, and re-layouts  1.8 us (3%)
  between operations  0.66 us (1%)
    pallas_call x4, Pallas kernels, plain_call(): pl.pallas_call(kernel, out_shape=[jax.ShapeDtypeStruct(shape, jnp.float32...  17.1 us
    pallas_call x1, Pallas kernels, opening(): pl.pallas_call(functools.partial(opening_kernel, mesh_shape), out_shape=[...  15.2 us
    pallas_call x1, Pallas kernels, field_step(): pl.pallas_call(electric_kernel, grid=(depth + 1,), out_shape=[jax.ShapeDt...  11.4 us
    all_to_all x1, starting transfers between devices, local(): lax.all_to_all(induced.reshape(segments, 1, tubes), AXES, split_axis=0, c...  6.17 us
    ppermute x2, starting transfers between devices, passed_round(): return lax.ppermute(value, axis, pairs)  3.22 us
    ppermute x2, waiting for transfers between devices, passed_round(): return lax.ppermute(value, axis, pairs)  3.13 us
    unnamed x6, local copies, waits for them, and re-layouts  1.8 us
  transfers between devices with their start and end apart: 3, of which 1 were waited for; matrix products, arithmetic and copies ran while one was open for 0% of the time, Pallas kernels for 16%

profile of v1, /device:TPU:0, one launch (start us, length us, event | category | flops | bytes accessed | tf_op | source)
XLA Modules:
  0.0 58.6 jit_solution(11859739966820401944)
XLA Ops:
  0.6 15.2 %opening.1 = (f32[32,128]{1,0:T(8,128)}, f32[2,1,128,256]{3,2,1,0:T(8,128)}, f32[2,1,128,256]{3,2,1,0:T(8,128)}, f32[32,32,128]{2,1,0:T(8,128)}) custom-call(s32[32,128]{1,0:T(8,128)} %bitcast.10, f32[3,32,128]{2,1,0:T(8,128)} %bitcast.8, f32[3,8,128,256]{3,2,1,0:T(8,128)} %electric_ref.1, f32[3,8,128,256]{3,2,1,0:T(8,128)} %magnetic_ref.1, ...), custom_call_target="tpu_custom_call" | custom-call | tf_op jit(solution)/shard_map/opening/pallas_call | solution.py:241
  15.8 5.6 %first_lines.1 = (f32[32,32,128]{2,1,0:T(8,128)}, f32[32,32,128]{2,1,0:T(8,128)}, f32[2,32,128]{2,1,0:T(8,128)}) custom-call(f32[32,128]{1,0:T(8,128)} %get-tuple-element.22.drive_ref, f32[32,32,128]{2,1,0:T(8,128)} %volts_ref.1, f32[32,32,128]{2,1,0:T(8,128)} %get-tuple-element.23.pre_ref, f32[32,32,128]{2,1,0:T(8,128)} %inductance_ref.5, ...), custom_call_target="tpu_custom_call" | custom-call | tf_op jit(solution)/shard_map/first_lines/pallas_call | solution.py:452
  21.5 2.9 %collective-permute-start = (f32[2,32,128]{2,1,0:T(8,128)}, f32[2,32,128]{2,1,0:T(8,128)S(1)}, u32[]{:S(2)}, u32[]{:S(2)}) collective-permute-start(f32[2,32,128]{2,1,0:T(8,128)} %get-tuple-element.24), channel_id=1, source_target_pairs={{0,1},{1,2},{2,3},{3,0},{4,5},{5,6},{6,7},{7,4},{8,9},{9,10},{10,1... | collective-permute-start | bytes 98312 | tf_op jit(solution)/shard_map/ppermute | solution.py:19
  24.4 5.4 %second_lines.1 = (f32[32,32,128]{2,1,0:T(8,128)}, f32[32,32,128]{2,1,0:T(8,128)}, f32[1,32,128]{2,1,0:T(8,128)}, f32[32,128]{1,0:T(8,128)}) custom-call(f32[32,128]{1,0:T(8,128)} %get-tuple-element.22.drive_ref, f32[32,32,128]{2,1,0:T(8,128)} %get-tuple-element.25.volts_ref, f32[32,32,128]{2,1,0:T(8,128)} %get-tuple-element.26.amps_ref, ...), custom_call_target="tpu_custom_call" | custom-call | tf_op jit(solution)/shard_map/second_lines/pallas_call | solution.py:452
  29.7 0.0 collective-permute-done.end_ref
  29.7 0.0 copy-start.1
  29.7 0.6 %copy-done.1 = f32[2,32,128]{2,1,0:T(8,128)} copy-done((f32[2,32,128]{2,1,0:T(8,128)}, f32[2,32,128]{2,1,0:T(8,128)S(1)}, u32[]{:S(2)}) %copy-start.1) | copy-done | bytes 32792
  30.4 2.2 %junction.1 = (f32[32,128]{1,0:T(8,128)}, f32[2,32,128]{2,1,0:T(8,128)}, f32[2,32,128]{2,1,0:T(8,128)}) custom-call(f32[2,32,128]{2,1,0:T(8,128)} %copy-done.1, s32[1,128]{1,0:T(1,128)} %bitcast.17, f32[32,32,128]{2,1,0:T(8,128)} %inductance_ref.5, f32[32,32,128]{2,1,0:T(8,128)} %capacitance_ref.7, f32[32,128]{1,0:T(8,128)} %get-tuple-element.27.total_ref), custom_call_target="tpu_custom_call" | custom-call | tf_op jit(solution)/shard_map/junction/pallas_call | solution.py:452
  32.5 6.2 %all-to-all-start = ((f32[32,1,128]{2,1,0:T(1,128)}), f32[32,1,128]{2,1,0:T(1,128)S(1)}, u32[]{:S(2)}, u32[]{:S(2)}) async-start(f32[32,1,128]{2,1,0:T(1,128)} %bitcast.13), calls=%async_computation | async-start | bytes 32768 | tf_op jit(solution)/shard_map/all_to_all | solution.py:613
  38.7 0.3 collective-permute-start.1
  39.0 3.1 %collective-permute-done.1.end_ref = f32[1,32,128]{2,1,0:T(8,128)S(1)} collective-permute-done((f32[1,32,128]{2,1,0:T(8,128)}, f32[1,32,128]{2,1,0:T(8,128)S(1)}, u32[]{:S(2)}, u32[]{:S(2)}) %collective-permute-start.1) | collective-permute-done | bytes 16416 | tf_op jit(solution)/shard_map/ppermute | solution.py:19
  42.1 0.0 copy-start.2
  42.1 0.6 %copy-done.2 = f32[1,32,128]{2,1,0:T(8,128)} copy-done((f32[1,32,128]{2,1,0:T(8,128)}, f32[1,32,128]{2,1,0:T(8,128)S(1)}, u32[]{:S(2)}) %copy-start.2) | copy-done | bytes 16408
  42.7 3.9 %last_lines.1 = (f32[32,32,128]{2,1,0:T(8,128)}, f32[32,32,128]{2,1,0:T(8,128)}) custom-call(f32[1,32,128]{2,1,0:T(8,128)} %copy-done.2, s32[1,128]{1,0:T(1,128)} %bitcast.18, f32[32,32,128]{2,1,0:T(8,128)} %get-tuple-element.34.volts_ref, f32[32,32,128]{2,1,0:T(8,128)} %get-tuple-element.35.amps_ref, f32[2,32,128]{2,1,0:T(8,128)} %get-tuple-element.36.volts_shift_ref, ...), custom_call_target="tpu_custom_call" | custom-call | tf_op jit(solution)/shard_map/last_lines/pallas_call | solution.py:452
  46.7 0.0 all-to-all-done
  46.7 0.0 copy-start
  46.7 0.6 %copy-done = f32[32,1,128]{2,1,0:T(1,128)} copy-done((f32[32,1,128]{2,1,0:T(1,128)}, f32[32,1,128]{2,1,0:T(1,128)S(1)}, u32[]{:S(2)}) %copy-start) | copy-done | bytes 16408
  47.3 11.4 %field_step.1 = (f32[3,8,128,256]{3,2,1,0:T(8,128)}, f32[3,8,128,256]{3,2,1,0:T(8,128)}) custom-call(s32[32,128]{1,0:T(8,128)} %bitcast.11, f32[3,32,128]{2,1,0:T(8,128)} %bitcast.9, f32[32,128]{1,0:T(8,128)} %bitcast.12, f32[3,8,128,256]{3,2,1,0:T(8,128)} %electric_ref.1, f32[3,8,128,256]{3,2,1,0:T(8,128)} %magnetic_ref.1, f32[8,128,256]{2,1,0:T(8,128)} %conductivity_ref.1, ...), custom_call_target="tpu_custom_call" | custom-call | tf_op jit(solution)/shard_map/field_step/pallas_call | solution.py:547
Async XLA Ops:
  21.5 8.3 %collective-permute-start = (f32[2,32,128]{2,1,0:T(8,128)}, f32[2,32,128]{2,1,0:T(8,128)S(1)}, u32[]{:S(2)}, u32[]{:S(2)}) collective-permute-start(f32[2,32,128]{2,1,0:T(8,128)} %get-tuple-element.24), channel_id=1, source_target_pairs={{0,1},{1,2},{2,3},{3,0},{4,5},{5,6},{6,7},{7,4},{8,9},{9,10},{10,1... | collective-permute-start | bytes 98312 | tf_op jit(solution)/shard_map/ppermute | solution.py:19
  29.7 0.6 %copy-start.1 = (f32[2,32,128]{2,1,0:T(8,128)}, f32[2,32,128]{2,1,0:T(8,128)S(1)}, u32[]{:S(2)}) copy-start(f32[2,32,128]{2,1,0:T(8,128)S(1)} %collective-permute-done.end_ref) | copy-start | bytes 98308
  32.5 14.1 %all-to-all-start = ((f32[32,1,128]{2,1,0:T(1,128)}), f32[32,1,128]{2,1,0:T(1,128)S(1)}, u32[]{:S(2)}, u32[]{:S(2)}) async-start(f32[32,1,128]{2,1,0:T(1,128)} %bitcast.13), calls=%async_computation | async-start | bytes 32768 | tf_op jit(solution)/shard_map/all_to_all | solution.py:613
  38.7 3.4 %collective-permute-start.1 = (f32[1,32,128]{2,1,0:T(8,128)}, f32[1,32,128]{2,1,0:T(8,128)S(1)}, u32[]{:S(2)}, u32[]{:S(2)}) collective-permute-start(f32[1,32,128]{2,1,0:T(8,128)} %get-tuple-element.33), channel_id=1, source_target_pairs={{0,1},{1,2},{2,3},{3,0},{4,5},{5,6},{6,7},{7,4},{8,9},{9,10},{10,1... | collective-permute-start | bytes 49160 | tf_op jit(solution)/shard_map/ppermute | solution.py:19
  42.1 0.6 %copy-start.2 = (f32[1,32,128]{2,1,0:T(8,128)}, f32[1,32,128]{2,1,0:T(8,128)S(1)}, u32[]{:S(2)}) copy-start(f32[1,32,128]{2,1,0:T(8,128)S(1)} %collective-permute-done.1.end_ref) | copy-start | bytes 49156
  46.7 0.6 %copy-start = (f32[32,1,128]{2,1,0:T(1,128)}, f32[32,1,128]{2,1,0:T(1,128)S(1)}, u32[]{:S(2)}) copy-start(f32[32,1,128]{2,1,0:T(1,128)S(1)} %all-to-all-done) | copy-start | bytes 49156

commit v2 on v1

--- a/solution.py
+++ b/solution.py
@@ -11,12 +11,6 @@
 LANES = 128
 SUBLANES = 8
 AXES = ("slab", "cable")
-
-
-def passed_round(value, axis, steps):
-    count = lax.axis_size(axis)
-    pairs = [(source, (source + steps) % count) for source in range(count)]
-    return lax.ppermute(value, axis, pairs)
 
 
 def params(*semantics):
@@ -116,10 +110,13 @@
 
 def opening_kernel(
     mesh_shape, cell_ref, tangent_ref, electric_hbm, magnetic_hbm, volts_hbm, amps_hbm,
-    inductance_hbm, drive_out, above_out, below_out, pre_out,
-    field, top_field, volts_ref, amps_ref, inductance_ref, push_ref, flat_ref,
-    send_ref, recv_ref, above_ref, top_ref, below_ref,
-    load_sem, send_sem, recv_sem, edge_sem,
+    inductance_hbm, capacitance_hbm, length_ref, link_ref,
+    above_out, below_out, induced_out, volts_out, amps_out,
+    field, top_field, volts_ref, amps_ref, inductance_ref, capacitance_ref, work_ref,
+    flat_ref, send_ref, recv_ref, send_back_ref, recv_back_ref, above_ref, top_ref,
+    below_ref, drive_ref, sum_ref, ends_ref, fed_ref, last_end_ref, last_fed_ref,
+    amps_shift_ref, volts_shift_ref, inflow_ref,
+    load_sem, send_sem, recv_sem, send_back_sem, recv_back_sem, edge_sem, feed_sem,
 ):
     depth, ny, nz = field.shape[1:]
     count, me, place = everyone(mesh_shape)
@@ -133,6 +130,7 @@
         (volts_hbm, volts_ref),
         (amps_hbm, amps_ref),
         (inductance_hbm, inductance_ref),
+        (capacitance_hbm, capacitance_ref),
     ]
     for i, (src, dst) in enumerate(extra):
         loads.append(pltpu.make_async_copy(src, dst, load_sem.at[depth + i]))
@@ -204,55 +202,131 @@
 
     for load in loads[depth + 1 :]:
         load.wait()
-    position = lax.broadcasted_iota(jnp.int32, volts_ref.shape[1:], 0)
-    set_push(volts_ref, None, push_ref, position)
+    position, live, last = line_positions(length_ref, volts_ref.shape[1])
+    conductors = volts_ref.shape[0]
+    set_push(volts_ref, None, work_ref, position)
 
     def keep(c, rows, total):
-        pre_out[c, rows, :] = amps_ref[c, rows, :] - total
-
-    contract(inductance_ref, push_ref, keep)
+        amps_ref[c, rows, :] = amps_ref[c, rows, :] - total
+
+    contract(inductance_ref, work_ref, keep)
+    total = inductance_ref[0]
+    for d in range(1, conductors):
+        total = total + inductance_ref[d]
+    sum_ref[...] = total
 
     recv_ref[me] = flat_ref[pl.ds(me, 1), :]
     above_out[:, 0] = above_ref[...]
     finish_rows()
     for row in range(count):
-        drive_out[row : row + 1, :] = recv_ref[row]
+        drive_ref[row : row + 1, :] = recv_ref[row]
+
+    def driven(c, carry):
+        row = pl.ds(c, 1)
+        new = live * (amps_ref[c] + sum_ref[row, :] * drive_ref[...])
+        amps_ref[c] = new
+        ends_ref[0, row, :] = jnp.sum(new * last, axis=0, keepdims=True)
+        return carry
+
+    lax.fori_loop(0, conductors, driven, 0, unroll=4)
+    set_slope(amps_ref, work_ref, position)
+    volts_substep(capacitance_ref, work_ref, volts_ref, volts_ref, live)
+    set_push(volts_ref, drive_ref, work_ref, position)
+    amps_substep(inductance_ref, work_ref, amps_ref, amps_ref, live, last, ends_ref, 1)
+
+    cables = mesh_shape[1]
+    fed_device = (
+        lax.axis_index("slab"),
+        (lax.axis_index("cable") + 1) % cables,
+    )
+    feeds = [
+        pltpu.make_async_remote_copy(
+            src_ref=src, dst_ref=dst, send_sem=feed_sem.at[2 * i], recv_sem=feed_sem.at[2 * i + 1],
+            device_id=fed_device, device_id_type=pl.DeviceIdType.MESH,
+        )
+        for i, (src, dst) in enumerate([(ends_ref, fed_ref), (last_end_ref, last_fed_ref)])
+    ]
+    feeds[0].start()
+    set_slope(amps_ref, work_ref, position)
+    volts_substep(capacitance_ref, work_ref, volts_ref, volts_ref, live)
+    set_push(volts_ref, drive_ref, work_ref, position)
+    amps_substep(inductance_ref, work_ref, amps_ref, amps_ref, live, last, last_end_ref, 0)
+    feeds[1].start()
+    feeds[0].wait()
+    junction(
+        fed_ref, link_ref, inductance_ref, capacitance_ref, amps_ref, flat_ref,
+        amps_shift_ref, volts_shift_ref,
+    )
+    for row in range(count):
+        send_back_ref[row] = flat_ref[row : row + 1, :]
+    start_back, finish_back = row_exchange(
+        count, me, place, send_back_ref, recv_back_ref, send_back_sem, recv_back_sem
+    )
+    start_back()
+    recv_back_ref[me] = flat_ref[pl.ds(me, 1), :]
+
+    def shifted(shift_ref, d):
+        row = pl.ds(d, 1)
+        return jnp.where(
+            position == 0, shift_ref[0, row, :],
+            jnp.where(position == 1, shift_ref[1, row, :], 0.0),
+        )
+
+    def settle(d, carry):
+        amps_out[d] = amps_ref[d] + shifted(amps_shift_ref, d)
+        volts_ref[d] = volts_ref[d] + shifted(volts_shift_ref, d)
+        return carry
+
+    lax.fori_loop(0, conductors, settle, 0, unroll=2)
+    feeds[1].wait()
+    inflow_ref[...] = feed(last_fed_ref[0], link_ref[...])
+    set_slope(amps_out, work_ref, position, inflow_ref)
+    volts_substep(capacitance_ref, work_ref, volts_ref, volts_out, live)
+
     below_here()
     below_out[:, 0] = below_ref[...]
     above_sent()
     below_sent()
-
-
-def opening(mesh_shape, cells, steer, electric, magnetic, volts, amps, inductance):
+    finish_back()
+    for row in range(count):
+        induced_out[row : row + 1, :] = recv_back_ref[row]
+
+
+def opening(
+    mesh_shape, cells, steer, electric, magnetic, volts, amps, inductance, capacitance,
+    length, link,
+):
     _, depth, ny, nz = electric.shape
     count = mesh_shape[0] * mesh_shape[1]
-    assert cells.shape[0] == count
+    conductors, segments, tubes = volts.shape
+    assert cells.shape[0] == count and segments == count and tubes == LANES
     vmem = pl.BlockSpec(memory_space=pltpu.VMEM)
     hbm = pl.BlockSpec(memory_space=pl.ANY)
     lines = volts.shape
+    matrix = inductance.shape
     row = (count, 1, LANES)
-    edge = (2, 1, ny, nz)
+    halo = (2, 1, ny, nz)
+    edge = (2, ny, nz)
+    end = (conductors, tubes)
+    rows = (segments, tubes)
     scratch = [
-        (3, depth, ny, nz), (2, ny, nz), lines, lines, inductance.shape, lines,
-        cells.shape, row, row, edge[:1] + edge[2:], edge[:1] + edge[2:],
-        edge[:1] + edge[2:],
+        (3, depth, ny, nz), edge, lines, lines, matrix, matrix, lines,
+        rows, row, row, row, row, edge, edge,
+        edge, rows, end, (2,) + end, (2,) + end, (1,) + end, (1,) + end,
+        (2,) + end, (2,) + end, end,
     ]
-    outs = [(lines[1], lines[2]), edge, edge, lines]
+    outs = [halo, halo, rows, lines, lines]
+    semaphores = [depth + 5, count, count, count, count, 4, 4]
     return pl.pallas_call(
         functools.partial(opening_kernel, mesh_shape),
         out_shape=[jax.ShapeDtypeStruct(shape, jnp.float32) for shape in outs],
-        in_specs=[vmem, vmem] + [hbm] * 5,
+        in_specs=[vmem, vmem] + [hbm] * 6 + [vmem, vmem],
         out_specs=[vmem] * len(outs),
         scratch_shapes=[pltpu.VMEM(shape, jnp.float32) for shape in scratch]
-        + [
-            pltpu.SemaphoreType.DMA((depth + 4,)),
-            pltpu.SemaphoreType.DMA((count,)),
-            pltpu.SemaphoreType.DMA((count,)),
-            pltpu.SemaphoreType.DMA((4,)),
-        ],
+        + [pltpu.SemaphoreType.DMA((number,)) for number in semaphores],
         compiler_params=pltpu.CompilerParams(collective_id=0, has_side_effects=True),
-        name="opening",
-    )(cells, steer, electric, magnetic, volts, amps, inductance)
+        name="lines_and_exchange",
+    )(cells, steer, electric, magnetic, volts, amps, inductance, capacitance, length, link)
 
 
 def ahead(x, axis):
@@ -342,45 +416,6 @@
     contract(capacitance_ref, slope_ref, finish)
 
 
-def first_lines_kernel(
-    drive_ref, volts_ref, pre_ref, inductance_ref, capacitance_ref, length_ref,
-    volts_out, amps_out, end_out, work_ref, mid_ref, sum_ref,
-):
-    position, live, last = line_positions(length_ref, volts_ref.shape[1])
-    total = inductance_ref[0]
-    for d in range(1, inductance_ref.shape[0]):
-        total = total + inductance_ref[d]
-    sum_ref[...] = total
-
-    def driven(c, carry):
-        row = pl.ds(c, 1)
-        new = live * (pre_ref[c] + sum_ref[row, :] * drive_ref[...])
-        mid_ref[c] = new
-        end_out[0, row, :] = jnp.sum(new * last, axis=0, keepdims=True)
-        return carry
-
-    lax.fori_loop(0, pre_ref.shape[0], driven, 0, unroll=4)
-    set_slope(mid_ref, work_ref, position)
-    volts_substep(capacitance_ref, work_ref, volts_ref, volts_out, live)
-    set_push(volts_out, drive_ref, work_ref, position)
-    amps_substep(inductance_ref, work_ref, mid_ref, amps_out, live, last, end_out, 1)
-
-
-def second_lines_kernel(
-    drive_ref, volts_ref, amps_ref, inductance_ref, capacitance_ref, length_ref,
-    volts_out, amps_out, end_out, total_out, work_ref,
-):
-    position, live, last = line_positions(length_ref, volts_ref.shape[1])
-    set_slope(amps_ref, work_ref, position)
-    volts_substep(capacitance_ref, work_ref, volts_ref, volts_out, live)
-    set_push(volts_out, drive_ref, work_ref, position)
-    amps_substep(inductance_ref, work_ref, amps_ref, amps_out, live, last, end_out, 0)
-    total = amps_out[0]
-    for c in range(1, amps_out.shape[0]):
-        total = total + amps_out[c]
-    total_out[...] = total
-
-
 def feed(end, link):
     picked = []
     for start in range(0, end.shape[0], SUBLANES):
@@ -398,8 +433,8 @@
     return total
 
 
-def junction_kernel(
-    end_ref, link_ref, inductance_ref, capacitance_ref, total_ref,
+def junction(
+    end_ref, link_ref, inductance_ref, capacitance_ref, amps_ref,
     induced_out, amps_shift_out, volts_shift_out,
 ):
     link = link_ref[...]
@@ -415,49 +450,14 @@
     volts_shift_out[1] = volts1
     amps_shift_out[0] = amps0
     amps_shift_out[1] = amps1
-    position = lax.broadcasted_iota(jnp.int32, total_ref.shape, 0)
-    conductors = end_ref.shape[1]
+    total = amps_ref[0]
+    for c in range(1, amps_ref.shape[0]):
+        total = total + amps_ref[c]
+    position = lax.broadcasted_iota(jnp.int32, total.shape, 0)
     first = jnp.sum(amps0, axis=0, keepdims=True)
     second = jnp.sum(amps1, axis=0, keepdims=True)
     shift = jnp.where(position == 0, first, jnp.where(position == 1, second, 0.0))
-    induced_out[...] = (total_ref[...] + shift) * (1.0 / conductors)
-
-
-def last_lines_kernel(
-    end_ref, link_ref, volts_ref, amps_ref, volts_shift_ref, amps_shift_ref,
-    capacitance_ref, length_ref, volts_out, amps_out, work_ref, inflow_ref, mid_ref,
-):
-    position, live, _ = line_positions(length_ref, volts_ref.shape[1])
-    inflow_ref[...] = feed(end_ref[0], link_ref[...])
-
-    def shifted(shift_ref, d):
-        row = pl.ds(d, 1)
-        return jnp.where(
-            position == 0, shift_ref[0, row, :],
-            jnp.where(position == 1, shift_ref[1, row, :], 0.0),
-        )
-
-    def one(d, carry):
-        amps_out[d] = amps_ref[d] + shifted(amps_shift_ref, d)
-        mid_ref[d] = volts_ref[d] + shifted(volts_shift_ref, d)
-        return carry
-
-    lax.fori_loop(0, volts_ref.shape[0], one, 0, unroll=2)
-    set_slope(amps_out, work_ref, position, inflow_ref)
-    volts_substep(capacitance_ref, work_ref, mid_ref, volts_out, live)
-
-
-def plain_call(kernel, outs, scratch, name, *operands):
-    vmem = pl.BlockSpec(memory_space=pltpu.VMEM)
-    return pl.pallas_call(
-        kernel,
-        out_shape=[jax.ShapeDtypeStruct(shape, jnp.float32) for shape in outs],
-        in_specs=[vmem] * len(operands),
-        out_specs=[vmem] * len(outs),
-        scratch_shapes=[pltpu.VMEM(shape, jnp.float32) for shape in scratch],
-        compiler_params=params(),
-        name=name,
-    )(*operands)
+    induced_out[...] = (total + shift) / amps_ref.shape[0]
 
 
 def electric_kernel(
@@ -584,41 +584,14 @@
     tube_length,
     junction_link,
 ):
-    conductors, segments, tubes = voltage.shape
     cells = sample_cell.reshape(-1, LANES)
     steer = tangent.reshape(3, -1, LANES)
-    length = tube_length[None, :]
-    link = junction_link[None, :]
-    lines = voltage.shape
-    end = (conductors, tubes)
-
-    drive, above, below, pre = opening(
-        mesh_shape, cells, steer, electric, magnetic, voltage, current, inverse_inductance
-    )
-    volts, amps, ends = plain_call(
-        first_lines_kernel, [lines, lines, (2,) + end], [lines, lines, end], "first_lines",
-        drive, voltage, pre, inverse_inductance, inverse_capacitance, length,
-    )
-    fed = passed_round(ends, "cable", 1)
-    volts, amps, ends, total = plain_call(
-        second_lines_kernel, [lines, lines, (1,) + end, (segments, tubes)], [lines],
-        "second_lines",
-        drive, volts, amps, inverse_inductance, inverse_capacitance, length,
-    )
-    fed_last = passed_round(ends, "cable", 1)
-    induced, amps_shift, volts_shift = plain_call(
-        junction_kernel, [(segments, tubes), (2,) + end, (2,) + end], [], "junction",
-        fed, link, inverse_inductance, inverse_capacitance, total,
-    )
-    induced_local = lax.all_to_all(
-        induced.reshape(segments, 1, tubes), AXES, split_axis=0, concat_axis=1, tiled=True
-    ).reshape(-1, LANES)
-    volts, amps = plain_call(
-        last_lines_kernel, [lines, lines], [lines, end, lines], "last_lines",
-        fed_last, link, volts, amps, volts_shift, amps_shift, inverse_capacitance, length,
+    above, below, induced, volts, amps = opening(
+        mesh_shape, cells, steer, electric, magnetic, voltage, current,
+        inverse_inductance, inverse_capacitance, tube_length[None, :], junction_link[None, :],
     )
     electric_new, magnetic_new = field_step(
-        electric, magnetic, conductivity, above, below, cells, steer, induced_local
+        electric, magnetic, conductivity, above, below, cells, steer, induced
     )
     return (electric_new, magnetic_new, volts, amps)
 

time: 59.2 us -> 42.2 us (0.71)
  starting transfers between devices: 9.39 us -> 0 us
  Pallas kernels: 43.7 us -> 39.5 us
  waiting for transfers between devices: 3.13 us -> 0 us
    pallas_call x4 -> x0, Pallas kernels: 17.1 us -> none  [plain_call(): pl.pallas_call(kernel, out_shape=[jax.ShapeDtypeStruct(shape, jnp.float32...]
    pallas_call x1, Pallas kernels: 15.2 us -> 28.1 us  [opening(): pl.pallas_call(functools.partial(opening_kernel, mesh_shape), out_shape=[...]
    all_to_all x1 -> x0, starting transfers between devices: 6.17 us -> none  [local(): lax.all_to_all(induced.reshape(segments, 1, tubes), AXES, split_axis=0, c...]
    ppermute x2 -> x0, starting transfers between devices: 3.22 us -> none  [passed_round(): return lax.ppermute(value, axis, pairs)]
    ppermute x2 -> x0, waiting for transfers between devices: 3.13 us -> none  [passed_round(): return lax.ppermute(value, axis, pairs)]
  transfers between devices with their start and end apart: 3 -> 0, of which waited for: 1 -> 0; matrix products, arithmetic and copies ran while one was open for 0% -> 0% of each run, Pallas kernels for 16% -> 0%
where the time goes in v2:
time: 42.2 us; the launch traced here: 41.8 us
  Pallas kernels  39.5 us (94%)
  local copies, waits for them, and re-layouts  1.59 us (4%)
  between operations  0.66 us (2%)
    pallas_call x1, Pallas kernels, opening(): pl.pallas_call(functools.partial(opening_kernel, mesh_shape), out_shape=[...  28.1 us
    pallas_call x1, Pallas kernels, field_step(): pl.pallas_call(electric_kernel, grid=(depth + 1,), out_shape=[jax.ShapeDt...  11.5 us
    unnamed x6, local copies, waits for them, and re-layouts  1.59 us

profile of v2, /device:TPU:0, one launch (start us, length us, event | category | flops | bytes accessed | tf_op | source)
XLA Modules:
  0.0 41.8 jit_solution(9499823863337039310)
XLA Ops:
  0.6 28.1 %lines_and_exchange.1 = (f32[2,1,128,256]{3,2,1,0:T(8,128)}, f32[2,1,128,256]{3,2,1,0:T(8,128)}, f32[32,128]{1,0:T(8,128)}, f32[32,32,128]{2,1,0:T(8,128)}, f32[32,32,128]{2,1,0:T(8,128)}) custom-call(s32[32,128]{1,0:T(8,128)} %bitcast.6, f32[3,32,128]{2,1,0:T(8,128)} %bitcast.4, f32[3,8,128,256]{3,2,1,0:T(8,128)} %electric_ref.1, ...), custom_call_target="tpu_custom_call" | custom-call | tf_op jit(solution)/shard_map/lines_and_exchange/pallas_call | solution.py:320
  28.7 0.0 copy-start.1
  28.7 0.0 copy-start
  28.7 11.5 %field_step.1 = (f32[3,8,128,256]{3,2,1,0:T(8,128)}, f32[3,8,128,256]{3,2,1,0:T(8,128)}) custom-call(s32[32,128]{1,0:T(8,128)} %bitcast.7, f32[3,32,128]{2,1,0:T(8,128)} %bitcast.5, f32[32,128]{1,0:T(8,128)} %get-tuple-element.11.induced_ref, f32[3,8,128,256]{3,2,1,0:T(8,128)} %electric_ref.1, f32[3,8,128,256]{3,2,1,0:T(8,128)} %magnetic_ref.1, ...), custom_call_target="tpu_custom_call" | custom-call | tf_op jit(solution)/shard_map/field_step/pallas_call | solution.py:547
  40.2 0.0 copy-done.1
  40.2 0.8 %copy.17 = f32[32,32,128]{2,1,0:T(8,128)} copy(f32[32,32,128]{2,1,0:T(8,128)S(1)} %copy-done.1) | data formatting | bytes 1048576
  41.0 0.0 copy-done
  41.0 0.8 %copy.18 = f32[32,32,128]{2,1,0:T(8,128)} copy(f32[32,32,128]{2,1,0:T(8,128)S(1)} %copy-done) | data formatting | bytes 1048576
Async XLA Ops:
  28.7 11.5 %copy-start.1 = (f32[32,32,128]{2,1,0:T(8,128)S(1)}, f32[32,32,128]{2,1,0:T(8,128)}, u32[]{:S(2)}) copy-start(f32[32,32,128]{2,1,0:T(8,128)} %get-tuple-element.24) | copy-start | bytes 1572868
  28.7 12.3 %copy-start = (f32[32,32,128]{2,1,0:T(8,128)S(1)}, f32[32,32,128]{2,1,0:T(8,128)}, u32[]{:S(2)}) copy-start(f32[32,32,128]{2,1,0:T(8,128)} %get-tuple-element.25) | copy-start | bytes 1572868

commit v3 on v2

--- a/solution.py
+++ b/solution.py
@@ -158,7 +158,7 @@
                 start = group * SUBLANES * halves + half
                 cells = cell_ref[pl.ds(start, SUBLANES, stride=halves), :]
                 low = cells & (SUBLANES - 1)
-                high = cells // SUBLANES - layer * (ny // SUBLANES)
+                high = (cells >> 3) - layer * (ny // SUBLANES)
 
                 def pick(chunk, found):
                     rows = pl.ds(pl.multiple_of(chunk * SUBLANES, SUBLANES), SUBLANES)
@@ -329,21 +329,30 @@
     )(cells, steer, electric, magnetic, volts, amps, inductance, capacitance, length, link)
 
 
+def at_edge(rolled, axis, last):
+    tile = LANES if axis == 1 else SUBLANES
+    extent = rolled.shape[axis]
+    cut = extent - tile if last else tile
+    first = lax.slice_in_dim(rolled, 0, cut, axis=axis)
+    second = lax.slice_in_dim(rolled, cut, extent, axis=axis)
+    edge = second if last else first
+    index = lax.broadcasted_iota(jnp.int32, edge.shape, axis)
+    edge = jnp.where(index == (tile - 1 if last else 0), 0.0, edge)
+    return jnp.concatenate([first, edge] if last else [edge, second], axis=axis)
+
+
 def ahead(x, axis):
-    extent = x.shape[axis]
-    index = lax.broadcasted_iota(jnp.int32, x.shape, axis)
-    return jnp.where(index == extent - 1, 0.0, pltpu.roll(x, extent - 1, axis)) - x
+    return at_edge(pltpu.roll(x, x.shape[axis] - 1, axis), axis, True) - x
 
 
 def behind(x, axis):
-    index = lax.broadcasted_iota(jnp.int32, x.shape, axis)
-    return x - jnp.where(index == 0, 0.0, pltpu.roll(x, 1, axis))
+    return x - at_edge(pltpu.roll(x, 1, axis), axis, False)
 
 
 def contract(matrix_ref, vector_ref, finish):
     conductors, segments = vector_ref.shape[0], vector_ref.shape[1]
     tall = 32 if segments % 32 == 0 else SUBLANES
-    wide = 4
+    wide = 8
 
     def block(i, carry):
         first = i * wide
@@ -462,8 +471,11 @@
 
 def electric_kernel(
     cell_ref, tangent_ref, induced_ref, electric_ref, magnetic_ref, conductivity_ref,
-    above_ref, below_ref, new_ref, fresh_ref, prev_ref, held_ref, merged_ref, tray_ref,
+    above_ref, below_ref, volts_ref, amps_ref, new_ref, fresh_ref, volts_out, amps_out,
+    prev_ref, held_ref, merged_ref, tray_ref,
 ):
+    volts_out[...] = volts_ref[...]
+    amps_out[...] = amps_ref[...]
     turn = pl.program_id(0)
     step = turn - 1
     ny, nz = new_ref.shape[2], new_ref.shape[3]
@@ -516,8 +528,8 @@
                 code = jnp.full((SUBLANES, LANES), trays, jnp.int32)
                 for tray in range(trays):
                     code = jnp.where(tray_ref[half, tray : tray + 1, :] == here, tray, code)
-                low = code % SUBLANES
-                group_of = code // SUBLANES
+                low = code & (SUBLANES - 1)
+                group_of = code >> 3
                 sigma = conductivity_ref[0, rows, lanes]
                 inverse = 1.0 / (1.0 + sigma)
                 keep = (1.0 - sigma) * inverse
@@ -537,17 +549,22 @@
         held_ref[...] = electric_ref[:, 0]
 
 
-def field_step(electric, magnetic, conductivity, above, below, cells, tangent, induced):
+def field_step(electric, magnetic, conductivity, above, below, cells, tangent, induced, volts, amps):
     _, depth, ny, nz = electric.shape
     halves = nz // LANES
     trays = cells.shape[0] // halves
     layer = (3, 1, ny, nz)
+    share = pl.cdiv(volts.shape[0], depth)
+    line = pl.BlockSpec(
+        (share,) + volts.shape[1:], lambda i: (jnp.maximum(i - 1, 0), 0, 0)
+    )
     leading = pl.BlockSpec(layer, lambda i: (0, jnp.minimum(i, depth - 1), 0, 0))
     trailing = pl.BlockSpec(layer, lambda i: (0, jnp.maximum(i - 1, 0), 0, 0))
     return pl.pallas_call(
         electric_kernel,
         grid=(depth + 1,),
-        out_shape=[jax.ShapeDtypeStruct(electric.shape, jnp.float32)] * 2,
+        out_shape=[jax.ShapeDtypeStruct(electric.shape, jnp.float32)] * 2
+        + [jax.ShapeDtypeStruct(volts.shape, jnp.float32)] * 2,
         in_specs=[
             whole_block(cells.shape),
             whole_block(tangent.shape),
@@ -557,8 +574,10 @@
             pl.BlockSpec((1, ny, nz), lambda i: (jnp.maximum(i - 1, 0), 0, 0)),
             whole_block(above.shape),
             whole_block(below.shape),
+            line,
+            line,
         ],
-        out_specs=[trailing, trailing],
+        out_specs=[trailing, trailing, line, line],
         scratch_shapes=[
             pltpu.VMEM((2, ny, nz), jnp.float32),
             pltpu.VMEM((3, ny, nz), jnp.float32),
@@ -567,7 +586,7 @@
         ],
         compiler_params=params("arbitrary"),
         name="field_step",
-    )(cells, tangent, induced, electric, magnetic, conductivity, above, below)
+    )(cells, tangent, induced, electric, magnetic, conductivity, above, below, volts, amps)
 
 
 def local(
@@ -590,8 +609,8 @@
         mesh_shape, cells, steer, electric, magnetic, voltage, current,
         inverse_inductance, inverse_capacitance, tube_length[None, :], junction_link[None, :],
     )
-    electric_new, magnetic_new = field_step(
-        electric, magnetic, conductivity, above, below, cells, steer, induced
+    electric_new, magnetic_new, volts, amps = field_step(
+        electric, magnetic, conductivity, above, below, cells, steer, induced, volts, amps
     )
     return (electric_new, magnetic_new, volts, amps)
 

time: 42.2 us -> 40.1 us (0.950)
  local copies, waits for them, and re-layouts: 1.59 us -> 0 us
  Pallas kernels: 39.5 us -> 39 us
    unnamed x6 -> x0, local copies, waits for them, and re-layouts: 1.59 us -> none
    pallas_call x1, Pallas kernels: 28.1 us -> 27.4 us  [opening(): pl.pallas_call(functools.partial(opening_kernel, mesh_shape), out_shape=[...]
where the time goes in v3:
time: 40.1 us; the launch traced here: 39.7 us
  Pallas kernels  39 us (97%)
  between operations  0.64 us (2%)
    pallas_call x1, Pallas kernels, opening(): pl.pallas_call(functools.partial(opening_kernel, mesh_shape), out_shape=[...  27.4 us
    pallas_call x1, Pallas kernels, field_step(): pl.pallas_call(electric_kernel, grid=(depth + 1,), out_shape=[jax.ShapeDt...  11.6 us

profile of v3, /device:TPU:0, one launch (start us, length us, event | category | flops | bytes accessed | tf_op | source)
XLA Modules:
  0.0 39.7 jit_solution(14552469121701958075)
XLA Ops:
  0.6 27.4 %lines_and_exchange.1 = (f32[2,1,128,256]{3,2,1,0:T(8,128)}, f32[2,1,128,256]{3,2,1,0:T(8,128)}, f32[32,128]{1,0:T(8,128)}, f32[32,32,128]{2,1,0:T(8,128)}, f32[32,32,128]{2,1,0:T(8,128)}) custom-call(s32[32,128]{1,0:T(8,128)} %bitcast.6, f32[3,32,128]{2,1,0:T(8,128)} %bitcast.4, f32[3,8,128,256]{3,2,1,0:T(8,128)} %electric_ref.1, ...), custom_call_target="tpu_custom_call" | custom-call | tf_op jit(solution)/shard_map/lines_and_exchange/pallas_call | solution.py:320
  28.1 11.6 %field_step.1 = (f32[3,8,128,256]{3,2,1,0:T(8,128)}, f32[3,8,128,256]{3,2,1,0:T(8,128)}, f32[32,32,128]{2,1,0:T(8,128)}, f32[32,32,128]{2,1,0:T(8,128)}) custom-call(s32[32,128]{1,0:T(8,128)} %bitcast.7, f32[3,32,128]{2,1,0:T(8,128)} %bitcast.5, f32[32,128]{1,0:T(8,128)} %get-tuple-element.9.induced_ref, f32[3,8,128,256]{3,2,1,0:T(8,128)} %electric_ref.1, ...), custom_call_target="tpu_custom_call" | custom-call | tf_op jit(solution)/shard_map/field_step/pallas_call | solution.py:563
